TPU v7x, 256 devices: a whole 4x4x8 slice. The times are simulated.
256 devices in a mesh: gx: 8 (over y_lo, x), gy: 32 (over y_hi, z, core).
Axes of the slice: x: 4, y: 4 (y_hi: 2, y_lo: 2; y = y_hi * 2 + y_lo), z: 8, core: 2. Of those that a mesh axis runs over, the one named last changes fastest.
Arguments:
- e_field: float32 [3, 128, 48, 4096], P(None, 'gx', None, 'gy'), may hold values from -6 to 6
- h_field: float32 [3, 128, 48, 4096], P(None, 'gx', None, 'gy'), may hold values from -6 to 6
- current: float32 [3, 128, 48, 4096], P(None, 'gx', None, 'gy'), may hold values from -3 to 3
- material: int32 [128, 48, 4096], P('gx', None, 'gy'), may hold values from 0 to 2
- pml_cells: int32 [2], replicated, may hold values from 8 to 16, as said below
- forward_field: bfloat16 [24, 128, 12, 4096], P(None, 'gx', None, 'gy'), may hold values from -2.5 to 2.5
- time_index: int32 [1], replicated, may hold values from 2 to 4095
Outputs:
- e_out: float32 [3, 128, 48, 4096], P(None, 'gx', None, 'gy')
- h_out: float32 [3, 128, 48, 4096], P(None, 'gx', None, 'gy')
- current_out: float32 [3, 128, 48, 4096], P(None, 'gx', None, 'gy')
- design_grad: float32 [128, 12, 4096], P('gx', None, 'gy')
Inputs may be any that keep to these rules, and one draw needn't show every extreme that they name: `material`: 0 is air, 1 dielectric, 2 Drude metal. `pml_cells`: exactly one of the two thicknesses equals 16.
All inputs are finite; a program needn't handle non-finite values.
Results may differ from a plain program's by a relative error of at most 0.0003.
Values sent between devices are 32-bit elements; how exact they have to be, the bound alone decides.
A program may use at most 64 MiB of HBM per device.

v0:
```python
import math

import jax
import jax.numpy as jnp
from jax import lax
from jax.sharding import PartitionSpec as P

DZ = 12
FREQ = 4
STEPS = 2
Z0 = 18


COURANT = 0.5
DIELECTRIC = 4.0
SIGMA_PEAK = 0.8
DRUDE_KEEP = 0.95 / 1.05
DRUDE_GAIN = 0.25 / 1.05
NUMERATORS = (3, 4, 5, 6)
PERIOD_STEPS = 64


def shifted(block, axis, distance):
    devices = range(lax.axis_size(axis))
    route = [((i - distance) % len(devices), i) for i in devices]
    return lax.ppermute(block, axis, route)


def absorber(pml_cells, z_cells):
    z_index = jnp.arange(z_cells, dtype=jnp.int32)
    low_cells = pml_cells[0]
    high_cells = pml_cells[1]
    low_depth = jnp.maximum(low_cells - z_index, 0).astype(jnp.float32) / low_cells.astype(
        jnp.float32
    )
    high_depth = jnp.maximum(z_index - (z_cells - 1 - high_cells), 0).astype(
        jnp.float32
    ) / high_cells.astype(jnp.float32)
    return (SIGMA_PEAK * (low_depth**3 + high_depth**3)).reshape((z_cells, 1))


def along_next(field_block, rim_plane, axis_id):
    extent = field_block.shape[axis_id]
    return jnp.concatenate(
        [lax.slice_in_dim(field_block, 1, extent, axis=axis_id), rim_plane], axis_id
    )


def along_prev(field_block, rim_plane, axis_id):
    extent = field_block.shape[axis_id]
    return jnp.concatenate(
        [rim_plane, lax.slice_in_dim(field_block, 0, extent - 1, axis=axis_id)], axis_id
    )


def edge_next(field_block, axis_id):
    return along_next(
        field_block, jnp.zeros_like(lax.slice_in_dim(field_block, 0, 1, axis=axis_id)), axis_id
    )


def edge_prev(field_block, axis_id):
    return along_prev(
        field_block, jnp.zeros_like(lax.slice_in_dim(field_block, 0, 1, axis=axis_id)), axis_id
    )


def z_next(field_block):
    return edge_next(field_block, field_block.ndim - 2)


def z_prev(field_block):
    return edge_prev(field_block, field_block.ndim - 2)


def h_update(h_now, e_now, next_vals, decay_z, h_scale):
    ey_xn, ez_xn, ex_yn, ez_yn = next_vals
    e_x, e_y, e_z = (e_now[0], e_now[1], e_now[2])
    curl_x = ez_yn - e_z - (z_next(e_y) - e_y)
    curl_y = z_next(e_x) - e_x - (ez_xn - e_z)
    curl_z = ey_xn - e_y - (ex_yn - e_x)
    return decay_z * h_now - h_scale * jnp.stack([curl_x, curl_y, curl_z])


def e_update(e_now, h_now, j_now, prev_vals, decay_z, e_scale, metal_mask):
    hy_xp, hz_xp, hx_yp, hz_yp = prev_vals
    h_x, h_y, h_z = (h_now[0], h_now[1], h_now[2])
    back_x = h_z - hz_yp - (h_y - z_prev(h_y))
    back_y = h_x - z_prev(h_x) - (h_z - hz_xp)
    back_z = h_y - hy_xp - (h_x - hx_yp)
    e_new = decay_z * e_now + e_scale * (jnp.stack([back_x, back_y, back_z]) - metal_mask * j_now)
    j_new = metal_mask * (DRUDE_KEEP * j_now + DRUDE_GAIN * e_new)
    return (e_new, j_new)


def phase_weights(forward_field, time_index):
    numerators = jnp.array(NUMERATORS, dtype=jnp.int32)
    levels = jnp.arange(STEPS, dtype=jnp.int32)
    tick_ids = time_index[0] - levels
    turn_ids = jnp.remainder(numerators[None, :] * tick_ids[:, None], PERIOD_STEPS)
    angles = turn_ids.astype(jnp.float32) * (2.0 * math.pi / PERIOD_STEPS)
    coeffs = jnp.stack([jnp.cos(angles), -jnp.sin(angles)], axis=-1)
    forward32 = forward_field.astype(jnp.float32).reshape((FREQ, 2, 3) + forward_field.shape[1:])
    return jnp.einsum("nfp,fpcxzy->ncxzy", coeffs, forward32, precision=lax.Precision.HIGHEST)


def level_grad(ex_centre, ey_centre, ez_centre, level_weights):
    return (
        ex_centre * level_weights[0] + ey_centre * level_weights[1] + ez_centre * level_weights[2]
    )


def body(e_field, h_field, current, material, pml_cells, forward_field, time_index):
    cells_x = e_field.shape[1]
    z_cells = e_field.shape[2]
    cells_y = e_field.shape[3]
    sigma_z = absorber(pml_cells, z_cells)
    half_loss = 1.0 + 0.5 * sigma_z
    decay_z = (1.0 - 0.5 * sigma_z) / half_loss
    h_scale = COURANT / half_loss
    weights = phase_weights(forward_field, time_index)
    grad_sum = jnp.zeros((cells_x, DZ, cells_y), jnp.float32)
    dielectric = (material == 1).astype(jnp.float32)
    metal_mask = (material == 2).astype(jnp.float32)
    e_scale = COURANT / ((1.0 + (DIELECTRIC - 1.0) * dielectric) * half_loss)
    e_now, h_now, j_now = (e_field, h_field, current)
    for level_idx in range(STEPS):
        lead_x = jnp.concatenate([e_now[1, :1], e_now[2, :1], e_now[0, :1, Z0 : Z0 + DZ]], 1)
        from_x = shifted(lead_x, "gx", -1)
        lead_y = jnp.concatenate(
            [e_now[0, :, :, :1], e_now[2, :, :, :1], e_now[1, :, Z0 : Z0 + DZ, :1]], 1
        )
        from_y = shifted(lead_y, "gy", -1)
        slab_e = e_now[:, :, Z0 : Z0 + DZ, :]
        ex_centre = 0.5 * (slab_e[0] + along_next(slab_e[0], from_x[:, 2 * z_cells :], 0))
        ey_centre = 0.5 * (slab_e[1] + along_next(slab_e[1], from_y[:, 2 * z_cells :], 2))
        ez_centre = 0.5 * (slab_e[2] + e_now[2, :, Z0 + 1 : Z0 + DZ + 1, :])
        grad_sum = grad_sum + level_grad(ex_centre, ey_centre, ez_centre, weights[level_idx])
        next_vals = (
            along_next(e_now[1], from_x[:, :z_cells], 0),
            along_next(e_now[2], from_x[:, z_cells : 2 * z_cells], 0),
            along_next(e_now[0], from_y[:, :z_cells], 2),
            along_next(e_now[2], from_y[:, z_cells : 2 * z_cells], 2),
        )
        h_now = h_update(h_now, e_now, next_vals, decay_z, h_scale)
        tail_x = jnp.concatenate([h_now[1, -1:], h_now[2, -1:]], 1)
        back_x = shifted(tail_x, "gx", 1)
        tail_y = jnp.concatenate([h_now[0, :, :, -1:], h_now[2, :, :, -1:]], 1)
        back_y = shifted(tail_y, "gy", 1)
        prev_vals = (
            along_prev(h_now[1], back_x[:, :z_cells], 0),
            along_prev(h_now[2], back_x[:, z_cells:], 0),
            along_prev(h_now[0], back_y[:, :z_cells], 2),
            along_prev(h_now[2], back_y[:, z_cells:], 2),
        )
        e_now, j_now = e_update(e_now, h_now, j_now, prev_vals, decay_z, e_scale, metal_mask)
    return (e_now, h_now, j_now, grad_sum)


def solution(mesh):
    placed = (
        P(None, "gx", None, "gy"),
        P(None, "gx", None, "gy"),
        P(None, "gx", None, "gy"),
        P("gx", None, "gy"),
        P(),
        P(None, "gx", None, "gy"),
        P(),
    )
    return jax.shard_map(
        body,
        mesh=mesh,
        in_specs=placed,
        out_specs=(
            P(None, "gx", None, "gy"),
            P(None, "gx", None, "gy"),
            P(None, "gx", None, "gy"),
            P("gx", None, "gy"),
        ),
        check_vma=False,
    )
```

profile of v0, /device:TPU:8, one launch (start us, length us, event | category | flops | bytes accessed | tf_op | source)
XLA Modules:
  0.0 102.8 jit_solution(10757514951193175419)
XLA Ops:
  0.7 1.3 %fusion.64 = (f32[1,16,48,1]{3,2,1,0:T(8,128)S(1)}, f32[1,16,48,1]{3,2,1,0:T(8,128)S(1)}) fusion(f32[3,16,48,128]{3,2,1,0:T(8,128)} %param.8), kind=kLoop, calls=%fused_computation.152 | loop fusion | bytes 12288 | tf_op jit(solution)/shard_map/slice | solution.py:131
  3.0 7.0 %collective-permute-start = (f32[16,108,1]{1,0,2:T(8,128)S(1)}, f32[16,108,1]{1,0,2:T(8,128)S(1)}, u32[]{:S(2)}, u32[]{:S(2)}) collective-permute-start(f32[16,108,1]{1,0,2:T(8,128)S(1)} %pad_maximum_fusion.5), channel_id=1, source_target_pairs={{1,0},{2,1},{3,2},{4,3},{5,4},{6,5},{7,6},{8,7},{9,8},{10,9},{11,1... | collective-permute-start | bytes 20744 | tf_op jit(solution)/shard_map/ppermute | solution.py:26
  10.7 3.5 %collective-permute-start.1 = (f32[1,108,128]{2,0,1:T(1,128)}, f32[1,108,128]{2,0,1:T(1,128)}, u32[]{:S(2)}, u32[]{:S(2)}) collective-permute-start(f32[1,108,128]{2,0,1:T(1,128)} %pad_maximum_fusion.1), channel_id=1, source_target_pairs={{32,0},{64,32},{96,64},{128,96},{160,128},{192,160},{224,192},{0,2... | collective-permute-start | bytes 165896 | tf_op jit(solution)/shard_map/ppermute | solution.py:26
  19.6 2.3 %convolution_bitcast_fusion = f32[2,3,16,12,128]{4,0,3,2,1:T(2,128)S(1)} fusion(bf16[4,2,3,16,12,128]{5,3,4,2,1,0:T(8,128)(2,1)S(1)} %bitcast.227, f32[2,4,1]{1,0,2:T(2,128)S(1)} %get-tuple-element.121, f32[2,4,1]{1,0,2:T(2,128)S(1)} %get-tuple-element.120), kind=kOutput, calls=%fused_computation | convolution fusion | flops 14155792 | bytes 1769536 | tf_op jit(solution)/shard_map/nfp,fpcxzy->ncxzy/dot_general | solution.py:104
  21.9 1.3 %fusion.66 = (f32[1,1,16,12,128]{4,0,3,2,1:T(1,128)}, f32[1,1,16,12,128]{4,0,3,2,1:T(1,128)}, f32[1,1,16,12,128]{4,0,3,2,1:T(1,128)}, f32[1,1,16,12,128]{4,0,3,2...) fusion(f32[2,3,16,12,128]{4,0,3,2,1:T(2,128)S(1)} %convolution_bitcast_fusion), kind=kLoop, calls=%fused_computation.154 | loop fusion | bytes 1179648 | tf_op jit(solution)/shard_map/slice | solution.py:109
  29.7 1.2 %slice_bitcast_fusion.18 = (f32[16,48,128]{2,1,0:T(8,128)S(1)}, f32[1,16,48,128]{3,2,1,0:T(8,128)S(1)}, f32[16,48,128]{2,1,0:T(8,128)S(1)}) fusion(f32[3,16,48,128]{3,2,1,0:T(8,128)S(1)} %copy-done.3, f32[1,16,48,1]{3,2,1,0:T(8,128)S(1)} %copy.449, f32[1,16,48,127]{3,2,1,0:T(8,128)S(1)} %slice_bitcast_fusion.9, f32[1,1,48,128]{3,2,1,0:T(8,128)S(1)} %bitcast.231, ...), kind=kLoop, calls=%fused_computation.72 | loop fusion | flops 491520 | bytes 3145728 | tf_op jit(solution)/shard_map/squeeze | solution.py:78
  32.4 1.1 %copy-done.24 = f32[3,16,48,128]{3,2,1,0:T(8,128)S(1)} copy-done((f32[3,16,48,128]{3,2,1,0:T(8,128)S(1)}, f32[3,16,48,128]{3,2,1,0:T(8,128)}, u32[]{:S(2)}) %copy-start.24) | copy-done | bytes 1179672
  35.0 1.0 fusion.63
  36.8 1.3 %copy.451 = f32[1,16,48,1]{2,1,3,0:T(8,128)S(1)} copy(f32[1,16,48,1]{3,1,2,0:T(8,128)} %get-tuple-element.83) | data formatting | bytes 6144 | tf_op jit(solution)/shard_map/slice | solution.py:148
  38.5 1.4 %pad_maximum_fusion.3 = f32[1,96,128]{2,0,1:T(1,128)} fusion(f32[1,48,128]{2,0,1:T(1,128)} %get-tuple-element.86, f32[1,48,128]{2,0,1:T(1,128)} %get-tuple-element.85), kind=kLoop, calls=%fused_computation.107 | loop fusion | flops 12288 | bytes 98304 | tf_op jit(solution)/shard_map/concatenate | solution.py:146
  40.0 1.3 %slice.527 = f32[1,12,128]{2,0,1:T(1,128)} slice(f32[1,108,128]{2,0,1:T(1,128)} %collective-permute-done.1), slice={[0:1], [96:108], [0:128]} | slice | bytes 12288 | tf_op jit(solution)/shard_map/slice | solution.py:135
  41.3 3.9 %collective-permute-done.2 = f32[16,96,1]{1,0,2:T(8,128)S(1)} collective-permute-done((f32[16,96,1]{1,0,2:T(8,128)S(1)}, f32[16,96,1]{1,0,2:T(8,128)S(1)}, u32[]{:S(2)}, u32[]{:S(2)}) %collective-permute-start.2) | collective-permute-done | bytes 6176 | tf_op jit(solution)/shard_map/ppermute | solution.py:26
  45.5 1.0 copy.453
  57.3 1.2 %copy.460 = f32[1,16,48,1]{2,1,3,0:T(8,128)S(1)} copy(f32[1,16,48,1]{3,1,2,0:T(8,128)} %get-tuple-element.72) | data formatting | bytes 6144 | tf_op jit(solution)/shard_map/slice | solution.py:131
  58.5 1.2 %copy.461 = f32[1,16,48,1]{2,1,3,0:T(8,128)S(1)} copy(f32[1,16,48,1]{3,1,2,0:T(8,128)} %get-tuple-element.73) | data formatting | bytes 6144 | tf_op jit(solution)/shard_map/slice | solution.py:131
  59.7 1.7 %copy.496 = f32[1,16,12,1]{2,1,3,0:T(8,128)} copy(f32[1,16,12,1]{3,1,2,0:T(8,128)} %slice.493) | data formatting | bytes 1536 | tf_op jit(solution)/shard_map/squeeze | solution.py:131
  62.2 4.2 %collective-permute-start.4 = (f32[16,108,1]{1,0,2:T(8,128)S(1)}, f32[16,108,1]{1,0,2:T(8,128)S(1)}, u32[]{:S(2)}, u32[]{:S(2)}) collective-permute-start(f32[16,108,1]{1,0,2:T(8,128)S(1)} %pad_maximum_fusion.7), channel_id=1, source_target_pairs={{1,0},{2,1},{3,2},{4,3},{5,4},{6,5},{7,6},{8,7},{9,8},{10,9},{11,1... | collective-permute-start | bytes 20744 | tf_op jit(solution)/shard_map/ppermute | solution.py:26
  66.4 1.9 %slice_bitcast_fusion.3 = f32[1,16,48,127]{3,1,2,0:T(8,128)} fusion(f32[16,48,128]{2,0,1:T(8,128)} %slice_bitcast_fusion.13), kind=kLoop, calls=%fused_computation.19 | loop fusion | bytes 780288 | tf_op jit(solution)/shard_map/concatenate | solution.py:44
  68.3 1.4 %pad_maximum_fusion.2 = f32[1,108,128]{2,0,1:T(1,128)} fusion(f32[1,12,128]{2,0,1:T(1,128)} %slice_bitcast_fusion.37, f32[1,48,128]{2,0,1:T(1,128)} %get-tuple-element.75, f32[1,48,128]{2,0,1:T(1,128)} %get-tuple-element.74), kind=kLoop, calls=%fused_computation.106 | loop fusion | flops 27648 | bytes 110592 | tf_op jit(solution)/shard_map/concatenate | solution.py:128
  71.2 1.7 %collective-permute-start.5 = (f32[1,108,128]{2,0,1:T(1,128)}, f32[1,108,128]{2,0,1:T(1,128)}, u32[]{:S(2)}, u32[]{:S(2)}) collective-permute-start(f32[1,108,128]{2,0,1:T(1,128)} %pad_maximum_fusion.2), channel_id=1, source_target_pairs={{32,0},{64,32},{96,64},{128,96},{160,128},{192,160},{224,192},{0,2... | collective-permute-start | bytes 165896 | tf_op jit(solution)/shard_map/ppermute | solution.py:26
  73.6 1.5 %copy.488 = f32[16,12,1]{2,0,1:T(8,128)} copy(f32[16,12,1]{1,0,2:T(8,128)} %slice.542) | data formatting | bytes 1536 | tf_op jit(solution)/shard_map/slice | solution.py:136
  75.2 1.0 copy.468
  76.1 1.0 copy.463
  77.9 1.5 %slice_bitcast_fusion.14 = (f32[16,48,128]{2,0,1:T(8,128)S(1)}, f32[1,16,48,128]{3,1,2,0:T(8,128)S(1)}, f32[16,48,128]{2,0,1:T(8,128)S(1)}) fusion(f32[3,16,48,128]{3,1,2,0:T(8,128)S(1)} %get-tuple-element.53, f32[1,16,48,1]{3,1,2,0:T(8,128)} %copy.468, f32[1,16,48,127]{3,1,2,0:T(8,128)} %slice_bitcast_fusion.3, ...), kind=kLoop, calls=%fused_computation.68 | loop fusion | flops 491520 | bytes 3145728 | tf_op jit(solution)/shard_map/squeeze | solution.py:78
  82.2 1.0 slice_bitcast_fusion.1
  86.1 2.2 %fusion.31 = f32[16,12,128]{2,0,1:T(8,128)} fusion(f32[3,16,48,128]{3,1,2,0:T(8,128)S(1)} %get-tuple-element.53, f32[3,16,48,128]{3,1,2,0:T(8,128)} %copy-done.13, f32[1,12,128]{2,0,1:T(1,128)} %slice.527, f32[15,12,128]{2,0,1:T(8,128)} %get-tuple-element.129, f32[16,12,1]{2,0,1:T(8,128)} %copy.482, f32[16,12,127]{2,0,1:T(8,128)} %slice.530, ...), kind=kLoop, calls=%fused_computation.79 | loop fusion | flops 663552 | bytes 1867776 | tf_op jit(solution)/shard_map/add | solution.py:138
  89.2 2.0 %collective-permute-done.6 = f32[16,96,1]{1,0,2:T(8,128)S(1)} collective-permute-done((f32[16,96,1]{1,0,2:T(8,128)S(1)}, f32[16,96,1]{1,0,2:T(8,128)S(1)}, u32[]{:S(2)}, u32[]{:S(2)}) %collective-permute-start.6) | collective-permute-done | bytes 6176 | tf_op jit(solution)/shard_map/ppermute | solution.py:26
  91.3 1.0 copy.475
  93.2 2.2 %collective-permute-done.7 = f32[1,96,128]{2,0,1:T(1,128)} collective-permute-done((f32[1,96,128]{2,0,1:T(1,128)}, f32[1,96,128]{2,0,1:T(1,128)}, u32[]{:S(2)}, u32[]{:S(2)}) %collective-permute-start.7) | collective-permute-done | bytes 49184 | tf_op jit(solution)/shard_map/ppermute | solution.py:26
  96.2 1.5 %slice_bitcast_fusion.12 = (f32[16,48,128]{2,0,1:T(8,128)S(1)}, f32[1,16,48,128]{3,1,2,0:T(8,128)S(1)}, f32[16,48,128]{2,0,1:T(8,128)S(1)}) fusion(f32[3,16,48,128]{3,1,2,0:T(8,128)S(1)} %copy-done.2, f32[1,16,48,127]{3,1,2,0:T(8,128)} %slice_bitcast_fusion, f32[1,16,48,1]{3,1,2,0:T(8,128)} %copy.475, f32[1,15,48,128]{3,1,2,0:T(8,128)} %get-tuple-element.60, ...), kind=kLoop, calls=%fused_computation.66 | loop fusion | flops 491520 | bytes 3145728 | tf_op jit(solution)/shard_map/squeeze | solution.py:87
  100.1 1.4 %copy.491 = f32[3,16,48,128]{3,2,1,0:T(8,128)} copy(f32[3,16,48,128]{3,1,2,0:T(8,128)S(1)} %get-tuple-element.49) | data formatting | bytes 2359296
  101.5 1.4 %copy.493 = f32[3,16,48,128]{3,2,1,0:T(8,128)} copy(f32[3,16,48,128]{3,1,2,0:T(8,128)S(1)} %get-tuple-element.48) | data formatting | bytes 2359296
  (177 shorter events, 40.4 us)
Async XLA Ops:
  0.6 19.0 %copy-start = (bf16[24,16,12,128]{3,1,2,0:T(8,128)(2,1)S(1)}, bf16[24,16,12,128]{3,1,2,0:T(8,128)(2,1)}, u32[]{:S(2)}) copy-start(bf16[24,16,12,128]{3,1,2,0:T(8,128)(2,1)} %param.13) | copy-start | bytes 3538948
  0.6 1.6 %copy-start.3 = (f32[3,16,48,128]{3,2,1,0:T(8,128)S(1)}, f32[3,16,48,128]{3,2,1,0:T(8,128)}, u32[]{:S(2)}) copy-start(f32[3,16,48,128]{3,2,1,0:T(8,128)} %param.8) | copy-start | bytes 3538948
  3.0 22.6 %collective-permute-start = (f32[16,108,1]{1,0,2:T(8,128)S(1)}, f32[16,108,1]{1,0,2:T(8,128)S(1)}, u32[]{:S(2)}, u32[]{:S(2)}) collective-permute-start(f32[16,108,1]{1,0,2:T(8,128)S(1)} %pad_maximum_fusion.5), channel_id=1, source_target_pairs={{1,0},{2,1},{3,2},{4,3},{5,4},{6,5},{7,6},{8,7},{9,8},{10,9},{11,1... | collective-permute-start | bytes 20744 | tf_op jit(solution)/shard_map/ppermute | solution.py:26
  10.7 18.3 %collective-permute-start.1 = (f32[1,108,128]{2,0,1:T(1,128)}, f32[1,108,128]{2,0,1:T(1,128)}, u32[]{:S(2)}, u32[]{:S(2)}) collective-permute-start(f32[1,108,128]{2,0,1:T(1,128)} %pad_maximum_fusion.1), channel_id=1, source_target_pairs={{32,0},{64,32},{96,64},{128,96},{160,128},{192,160},{224,192},{0,2... | collective-permute-start | bytes 165896 | tf_op jit(solution)/shard_map/ppermute | solution.py:26
  14.3 3.6 %copy-start.14 = (s32[16,48,128]{2,1,0:T(8,128)S(1)}, s32[16,48,128]{2,1,0:T(8,128)}, u32[]{:S(2)}) copy-start(s32[16,48,128]{2,1,0:T(8,128)} %param.11) | copy-start | bytes 1179652
  17.9 1.5 %copy-start.40 = (s32[4]{0:T(128)S(1)}, s32[4]{0:T(128)}, u32[]{:S(2)}) copy-start(s32[4]{0:T(128)} %constant.48.clone) | copy-start | bytes 52
  36.8 3.1 %copy-start.12 = (f32[16,48,128]{2,0,1:T(8,128)}, f32[16,48,128]{2,0,1:T(8,128)S(1)}, u32[]{:S(2)}) copy-start(f32[16,48,128]{2,0,1:T(8,128)S(1)} %slice_bitcast_fusion.15) | copy-start | bytes 1179652
  38.5 6.7 %collective-permute-start.2 = (f32[16,96,1]{1,0,2:T(8,128)S(1)}, f32[16,96,1]{1,0,2:T(8,128)S(1)}, u32[]{:S(2)}, u32[]{:S(2)}) collective-permute-start(f32[16,96,1]{1,0,2:T(8,128)S(1)} %pad_maximum_fusion.6), channel_id=1, source_target_pairs={{31,0},{0,1},{1,2},{2,3},{3,4},{4,5},{5,6},{6,7},{7,8},{8,9},{9,10... | collective-permute-start | bytes 18440 | tf_op jit(solution)/shard_map/ppermute | solution.py:26
  40.0 6.5 %collective-permute-start.3 = (f32[1,96,128]{2,0,1:T(1,128)}, f32[1,96,128]{2,0,1:T(1,128)}, u32[]{:S(2)}, u32[]{:S(2)}) collective-permute-start(f32[1,96,128]{2,0,1:T(1,128)} %pad_maximum_fusion.3), channel_id=1, source_target_pairs={{224,0},{0,32},{32,64},{64,96},{96,128},{128,160},{160,192},{192,2... | collective-permute-start | bytes 147464 | tf_op jit(solution)/shard_map/ppermute | solution.py:26
  48.5 1.6 %copy-start.5 = (f32[3,16,48,128]{3,2,1,0:T(8,128)S(1)}, f32[3,16,48,128]{3,2,1,0:T(8,128)}, u32[]{:S(2)}) copy-start(f32[3,16,48,128]{3,2,1,0:T(8,128)} %param.10) | copy-start | bytes 3538948
  48.5 1.7 %copy-start.7 = (f32[16,48,128]{2,0,1:T(8,128)S(1)}, f32[16,48,128]{2,0,1:T(8,128)}, u32[]{:S(2)}) copy-start(f32[16,48,128]{2,0,1:T(8,128)} %copy.440) | copy-start | bytes 1179652
  48.5 1.8 %copy-start.9 = (f32[16,48,128]{2,0,1:T(8,128)S(1)}, f32[16,48,128]{2,0,1:T(8,128)}, u32[]{:S(2)}) copy-start(f32[16,48,128]{2,0,1:T(8,128)} %copy.458) | copy-start | bytes 1179652
  48.5 1.8 %copy-start.34 = (f32[48]{0:T(128)S(1)}, f32[48]{0:T(128)}, u32[]{:S(2)}) copy-start(f32[48]{0:T(128)} %get-tuple-element.122) | copy-start | bytes 580
  51.3 3.6 %copy-start.13 = (f32[3,16,48,128]{3,1,2,0:T(8,128)}, f32[3,16,48,128]{3,1,2,0:T(8,128)S(1)}, u32[]{:S(2)}) copy-start(f32[3,16,48,128]{3,1,2,0:T(8,128)S(1)} %get-tuple-element.52) | copy-start | bytes 3538948
  61.4 8.3 %copy-start.30 = (f32[16,12,128]{2,0,1:T(8,128)S(1)}, f32[16,12,128]{2,0,1:T(8,128)}, u32[]{:S(2)}) copy-start(f32[16,12,128]{2,0,1:T(8,128)} %get-tuple-element.127) | copy-start | bytes 294916
  61.4 9.1 %copy-start.29 = (f32[16,12,128]{2,0,1:T(8,128)S(1)}, f32[16,12,128]{2,0,1:T(8,128)}, u32[]{:S(2)}) copy-start(f32[16,12,128]{2,0,1:T(8,128)} %get-tuple-element.126) | copy-start | bytes 294916
  62.2 10.7 %collective-permute-start.4 = (f32[16,108,1]{1,0,2:T(8,128)S(1)}, f32[16,108,1]{1,0,2:T(8,128)S(1)}, u32[]{:S(2)}, u32[]{:S(2)}) collective-permute-start(f32[16,108,1]{1,0,2:T(8,128)S(1)} %pad_maximum_fusion.7), channel_id=1, source_target_pairs={{1,0},{2,1},{3,2},{4,3},{5,4},{6,5},{7,6},{8,7},{9,8},{10,9},{11,1... | collective-permute-start | bytes 20744 | tf_op jit(solution)/shard_map/ppermute | solution.py:26
  71.2 6.0 %collective-permute-start.5 = (f32[1,108,128]{2,0,1:T(1,128)}, f32[1,108,128]{2,0,1:T(1,128)}, u32[]{:S(2)}, u32[]{:S(2)}) collective-permute-start(f32[1,108,128]{2,0,1:T(1,128)} %pad_maximum_fusion.2), channel_id=1, source_target_pairs={{32,0},{64,32},{96,64},{128,96},{160,128},{192,160},{224,192},{0,2... | collective-permute-start | bytes 165896 | tf_op jit(solution)/shard_map/ppermute | solution.py:26
  81.6 1.7 %copy-start.1 = (f32[3,16,48,128]{3,1,2,0:T(8,128)}, f32[3,16,48,128]{3,1,2,0:T(8,128)S(1)}, u32[]{:S(2)}) copy-start(f32[3,16,48,128]{3,1,2,0:T(8,128)S(1)} %fusion.2) | copy-start | bytes 3538948
  83.3 2.8 %copy-start.11 = (f32[16,48,128]{2,0,1:T(8,128)}, f32[16,48,128]{2,0,1:T(8,128)S(1)}, u32[]{:S(2)}) copy-start(f32[16,48,128]{2,0,1:T(8,128)S(1)} %slice_bitcast_fusion.11) | copy-start | bytes 1179652
  84.2 1.9 %copy-start.25 = (f32[1,1,16,12,128]{4,0,3,2,1:T(1,128)S(1)}, f32[1,1,16,12,128]{4,0,3,2,1:T(1,128)}, u32[]{:S(2)}) copy-start(f32[1,1,16,12,128]{4,0,3,2,1:T(1,128)} %get-tuple-element.98) | copy-start | bytes 294916
  84.2 1.9 %copy-start.26 = (f32[1,1,16,12,128]{4,0,3,2,1:T(1,128)S(1)}, f32[1,1,16,12,128]{4,0,3,2,1:T(1,128)}, u32[]{:S(2)}) copy-start(f32[1,1,16,12,128]{4,0,3,2,1:T(1,128)} %get-tuple-element.99) | copy-start | bytes 294916
  84.2 1.9 %copy-start.27 = (f32[1,1,16,12,128]{4,0,3,2,1:T(1,128)S(1)}, f32[1,1,16,12,128]{4,0,3,2,1:T(1,128)}, u32[]{:S(2)}) copy-start(f32[1,1,16,12,128]{4,0,3,2,1:T(1,128)} %get-tuple-element.100) | copy-start | bytes 294916
  84.2 1.9 %copy-start.28 = (f32[1,1,16,12,128]{4,0,3,2,1:T(1,128)S(1)}, f32[1,1,16,12,128]{4,0,3,2,1:T(1,128)}, u32[]{:S(2)}) copy-start(f32[1,1,16,12,128]{4,0,3,2,1:T(1,128)} %get-tuple-element.101) | copy-start | bytes 294916
  84.5 6.7 %collective-permute-start.6 = (f32[16,96,1]{1,0,2:T(8,128)S(1)}, f32[16,96,1]{1,0,2:T(8,128)S(1)}, u32[]{:S(2)}, u32[]{:S(2)}) collective-permute-start(f32[16,96,1]{1,0,2:T(8,128)S(1)} %pad_maximum_fusion.8), channel_id=1, source_target_pairs={{31,0},{0,1},{1,2},{2,3},{3,4},{4,5},{5,6},{6,7},{7,8},{8,9},{9,10... | collective-permute-start | bytes 18440 | tf_op jit(solution)/shard_map/ppermute | solution.py:26
  85.3 2.9 %copy-start.31 = (f32[1,1,48,128]{3,2,1,0:T(8,128)S(1)}, f32[1,1,48,128]{3,2,1,0:T(8,128)}, u32[]{:S(2)}) copy-start(f32[1,1,48,128]{3,2,1,0:T(8,128)} %get-tuple-element.63) | copy-start | bytes 73732
  85.3 2.9 %copy-start.32 = (f32[1,1,48,128]{3,2,1,0:T(8,128)S(1)}, f32[1,1,48,128]{3,2,1,0:T(8,128)}, u32[]{:S(2)}) copy-start(f32[1,1,48,128]{3,2,1,0:T(8,128)} %get-tuple-element.64) | copy-start | bytes 73732
  88.2 8.0 %copy-start.2 = (f32[3,16,48,128]{3,1,2,0:T(8,128)S(1)}, f32[3,16,48,128]{3,1,2,0:T(8,128)}, u32[]{:S(2)}) copy-start(f32[3,16,48,128]{3,1,2,0:T(8,128)} %copy-done.1) | copy-start | bytes 3538948
  88.9 6.5 %collective-permute-start.7 = (f32[1,96,128]{2,0,1:T(1,128)}, f32[1,96,128]{2,0,1:T(1,128)}, u32[]{:S(2)}, u32[]{:S(2)}) collective-permute-start(f32[1,96,128]{2,0,1:T(1,128)} %pad_maximum_fusion.4), channel_id=1, source_target_pairs={{224,0},{0,32},{32,64},{64,96},{96,128},{128,160},{160,192},{192,2... | collective-permute-start | bytes 147464 | tf_op jit(solution)/shard_map/ppermute | solution.py:26
  96.2 1.6 %slice-start = ((f32[16,48,128]{2,0,1:T(8,128)}), f32[16,47,128]{2,0,1:T(8,128)S(1)}, s32[]{:S(2)}) async-start(f32[16,48,128]{2,0,1:T(8,128)} %copy-done.11), calls=%async_computation | async-start | bytes 770048 | tf_op jit(solution)/shard_map/slice | solution.py:52
  96.2 1.6 %copy-start.17 = (f32[16,48,1]{2,0,1:T(8,128)S(1)}, f32[16,48,1]{2,0,1:T(8,128)}, u32[]{:S(2)}) copy-start(f32[16,48,1]{2,0,1:T(8,128)} %copy.471) | copy-start | bytes 9220
  96.2 1.6 %copy-start.19 = (f32[15,48,128]{2,0,1:T(8,128)S(1)}, f32[15,48,128]{2,0,1:T(8,128)}, u32[]{:S(2)}) copy-start(f32[15,48,128]{2,0,1:T(8,128)} %get-tuple-element.59) | copy-start | bytes 1105924
  (20 other events, 23.1 us)
where the time goes:
time: 104 us; the launch traced here: 103 us
  local copies, waits for them, and re-layouts  54.4 us (52%)
  other arithmetic  17.4 us (17%)
  starting transfers between devices  16.8 us (16%)
  waiting for transfers between devices  8.11 us (8%)
  between operations  3.76 us (4%)
  matrix products  2.33 us (2%)
    ppermute x8, starting transfers between devices, shifted(): return lax.ppermute(block, axis, route)  16.8 us
    unnamed x87, local copies, waits for them, and re-layouts  9.03 us
    ppermute x8, waiting for transfers between devices, shifted(): return lax.ppermute(block, axis, route)  8.11 us
    slice x12, local copies, waits for them, and re-layouts, along_next(): lax.slice_in_dim(field_block, 1, extent, axis=axis_id)  5.19 us
    concatenate x4, local copies, waits for them, and re-layouts, along_next(): jnp.concatenate([lax.slice_in_dim(field_block, 1, extent, axis=axis_id),...  3.94 us
    slice x3, local copies, waits for them, and re-layouts, body(): e_now[0, :, :, :1]  3.44 us
    slice x6, local copies, waits for them, and re-layouts, body(): tail_y = jnp.concatenate([h_now[0, :, :, -1:], h_now[2, :, :, -1:]], 1)  3.28 us
    slice x4, local copies, waits for them, and re-layouts, body(): from_y[:, 2 * z_cells:]  3.11 us
  transfers between devices with their start and end apart: 8, of which 3 were waited for; matrix products, arithmetic and copies ran while one was open for 31% of the time, Pallas kernels for 0%

commit v1 on v0

v1 whole, which is shorter than its diff:
```python
import functools
import math

import jax
import jax.numpy as jnp
from jax import lax
from jax.experimental import pallas as pl
from jax.experimental.pallas import tpu as pltpu
from jax.sharding import PartitionSpec as P

Z = 48
DZ = 12
FREQ = 4
STEPS = 2
Z0 = 18
W0 = 16
WN = 16
OFF = Z0 - W0
YL = 128
GAP = 16

COURANT = 0.5
SIGMA_PEAK = 0.8
DRUDE_KEEP = 0.95 / 1.05
DRUDE_GAIN = 0.25 / 1.05
PERIOD_STEPS = 64
F32 = jnp.float32
MESH = pl.DeviceIdType.MESH


def lanes():
    return lax.broadcasted_iota(jnp.int32, (Z, YL), 1)


def rows():
    return lax.broadcasted_iota(jnp.int32, (Z, YL), 0)


def z_next(v):
    return jnp.where(rows() == Z - 1, 0.0, pltpu.roll(v, Z - 1, 0))


def z_prev(v):
    return jnp.where(rows() == 0, 0.0, pltpu.roll(v, 1, 0))


def absorber(pml):
    low = pml[0]
    high = pml[1]
    z = rows()
    low_depth = jnp.maximum(low - z, 0).astype(F32) / low.astype(F32)
    high_depth = jnp.maximum(z - (Z - 1 - high), 0).astype(F32) / high.astype(F32)
    sigma = SIGMA_PEAK * (low_depth * low_depth * low_depth + high_depth * high_depth * high_depth)
    half_loss = 1.0 + 0.5 * sigma
    return (1.0 - 0.5 * sigma) / half_loss, COURANT / half_loss


def phase_table(tick):
    lane = lax.broadcasted_iota(jnp.int32, (8, YL), 1)
    level = lane // 8
    freq = (lane % 8) // 2
    turn = ((3 + freq) * (tick[0] - level)) & (PERIOD_STEPS - 1)
    angle = turn.astype(F32) * (2.0 * math.pi / PERIOD_STEPS)
    return jnp.where(lane % 2 == 0, jnp.cos(angle), -jnp.sin(angle))


def h_partial(x, e, h, h_out, decay, scale, packs):
    lane = lanes()
    ex, ey, ez = e[0, x], e[1, x], e[2, x]
    last = lane == YL - 1
    ez_yn = jnp.where(last, 0.0, pltpu.roll(ez, YL - 1, 1))
    ex_yn = jnp.where(last, 0.0, pltpu.roll(ex, YL - 1, 1))
    hx = decay * h[0, x] - scale * (ez_yn - ez - (z_next(ey) - ey))
    hy = decay * h[1, x] - scale * (z_next(ex) - ex - (e[2, x + 1] - ez))
    hz = decay * h[2, x] - scale * (e[1, x + 1] - ey - (ex_yn - ex))
    h_out[0, x] = hx
    h_out[1, x] = hy
    h_out[2, x] = hz
    first_cols, last_cols = packs
    for group, v in enumerate((ex, ez, ey)):
        at = GAP * group + x
        first_cols = jnp.where(lane == at, pltpu.roll(v, at, 1), first_cols)
    for group, v in enumerate((hx, hz)):
        at = GAP * group + x
        last_cols = jnp.where(lane == at, pltpu.roll(v, at + 1, 1), last_cols)
    return first_cols, last_cols


def rims(e, pack_e, in_x, in_y, diag_e, diag_h, scale):
    lane = lanes()
    hy = in_x[0] + scale * e[2, 0]
    corner = jnp.where(lane == YL - 1, pltpu.roll(diag_e, YL - GAP, 1), 0.0)
    hz = in_x[1] + scale * (corner - e[1, 0])
    term = jnp.where(
        lane < GAP,
        -pltpu.roll(pack_e, YL - GAP, 1),
        jnp.where(lane < 2 * GAP, pltpu.roll(pack_e, GAP, 1), 0.0),
    )
    return hy, hz, in_y, term


def e_update(x, prev, hp, e, j, mat, col_e, col_h, decay, scale, outs):
    lane = lanes()
    e_out, h_out, j_out = outs
    hy_xp, hz_xp = prev
    last = lane == YL - 1
    first = lane == 0
    ex_halo = pltpu.roll(col_e, YL - 1 - x, 1)
    ez_halo = pltpu.roll(col_e, YL - 1 - GAP - x, 1)
    hx = hp[0, x] - jnp.where(last, scale * ez_halo, 0.0)
    hy = hp[1, x]
    hz = hp[2, x] + jnp.where(last, scale * ex_halo, 0.0)
    h_out[0, x] = hx
    h_out[1, x] = hy
    h_out[2, x] = hz
    hx_yp = jnp.where(first, pltpu.roll(col_h, YL - x, 1), pltpu.roll(hx, 1, 1))
    hz_yp = jnp.where(first, pltpu.roll(col_h, YL - GAP - x, 1), pltpu.roll(hz, 1, 1))
    m = mat[x]
    metal = m == 2
    e_scale = scale * jnp.where(m == 1, 0.25, 1.0)
    backs = (
        hz - hz_yp - (hy - z_prev(hy)),
        hx - z_prev(hx) - (hz - hz_xp),
        hy - hy_xp - (hx - hx_yp),
    )
    for c, back in enumerate(backs):
        j_now = j[c, x]
        e_new = decay * e[c, x] + e_scale * (back - jnp.where(metal, j_now, 0.0))
        e_out[c, x] = e_new
        j_out[c, x] = jnp.where(metal, DRUDE_KEEP * j_now + DRUDE_GAIN * e_new, 0.0)
    return hy, hz


def window_grad(x, e, col_e, w, level):
    lane = lax.broadcasted_iota(jnp.int32, (WN, YL), 1)
    win = pl.ds(W0, WN)
    ex, ey, ez = e[0, x, win], e[1, x, win], e[2, x, win]
    ex_xn = e[0, x + 1, win]
    halo = pltpu.roll(col_e, YL - 1 - 2 * GAP - x, 1)
    ey_yn = jnp.where(lane == YL - 1, halo, pltpu.roll(ey, YL - 1, 1))
    ez_zn = e[2, x, pl.ds(W0 + 1, WN)]
    return 0.5 * (
        (ex + ex_xn) * w[level, 0, x] + (ey + ey_yn) * w[level, 1, x] + (ez + ez_zn) * w[level, 2, x]
    )


def exchange_kernel(
    gx, gy, nx,
    pml, tick, e_in, h_in, j_in, m_in, f_in,
    e1, h1, j1, mat, w, grad, coef, rim_x, col_e_out, col_h_out,
    e0, hp, j0, fwd, pack_e, pack_h, send_h, got_e, got_slab, got_h, got_ye, got_yh, got_de, got_dh,
    load_sem, send_sem, recv_sem,
):
    me_x = lax.axis_index("gx")
    me_y = lax.axis_index("gy")
    x_next, x_prev = lax.rem(me_x + 1, gx), lax.rem(me_x + gx - 1, gx)
    y_next, y_prev = lax.rem(me_y + 1, gy), lax.rem(me_y + gy - 1, gy)
    barrier = pltpu.get_barrier_semaphore()
    peers = (
        (x_prev, me_y), (x_next, me_y), (me_x, y_prev), (me_x, y_next), (x_next, y_prev), (x_prev, y_next),
    )
    for peer in peers:
        pl.semaphore_signal(barrier, inc=1, device_id=peer, device_id_type=MESH)

    loads = [
        pltpu.make_async_copy(e_in, e0.at[:, pl.ds(0, nx)], load_sem.at[0]),
        pltpu.make_async_copy(h_in, hp, load_sem.at[1]),
        pltpu.make_async_copy(f_in, fwd, load_sem.at[2]),
        pltpu.make_async_copy(j_in, j0, load_sem.at[3]),
        pltpu.make_async_copy(m_in, mat, load_sem.at[4]),
    ]
    for load in loads:
        load.start()

    lane = lanes()
    decay, scale = absorber(pml)
    coef[0] = decay
    coef[1] = scale
    zero = jnp.zeros((Z, YL), F32)
    for c in range(3):
        e0[c, nx] = zero
        e1[c, nx] = zero

    def send(level, e):
        routes = (
            (e.at[pl.ds(1, 2), 0], got_e.at[level]),
            (e.at[0, 0, pl.ds(W0, WN)], got_slab.at[level]),
            (send_h.at[level], got_h.at[level]),
            (pack_e.at[level], got_ye.at[level]),
            (pack_h.at[level], got_yh.at[level]),
            (pack_e.at[level], got_de.at[level]),
            (pack_h.at[level], got_dh.at[level]),
        )
        targets = (peers[0], peers[0], peers[1], peers[2], peers[3], peers[4], peers[5])
        copies = []
        for i, ((src, dst), peer) in enumerate(zip(routes, targets)):
            copies.append(
                pltpu.make_async_remote_copy(
                    src_ref=src,
                    dst_ref=dst,
                    send_sem=send_sem.at[level, i],
                    recv_sem=recv_sem.at[level, i],
                    device_id=peer,
                    device_id_type=MESH,
                )
            )
        for copy in copies:
            copy.start()
        return copies

    def prepare(level, e, h, h_out):
        def plane(x, packs):
            return h_partial(x, e, h, h_out, coef[0], coef[1], packs)

        first_cols, last_cols = lax.fori_loop(0, nx, plane, (zero, zero))
        last_cols = jnp.where(lane == 2 * GAP, pltpu.roll(e[1, 0], 2 * GAP + 1, 1), last_cols)
        pack_e[level] = first_cols
        pack_h[level] = last_cols
        send_h[level, 0] = h_out[1, nx - 1]
        send_h[level, 1] = h_out[2, nx - 1]

    def receive(level, e, h):
        e[0, nx, pl.ds(W0, WN)] = got_slab[level]
        h[1, nx - 1] = h[1, nx - 1] + scale * got_e[level, 1]
        h[2, nx - 1] = h[2, nx - 1] - scale * got_e[level, 0]
        corner = jnp.where(lane == YL - 1, pltpu.roll(got_de[level], YL - nx, 1), 0.0)
        hy = got_h[level, 0] + scale * e[2, 0]
        hz = got_h[level, 1] + scale * (corner - e[1, 0])
        own = pack_e[level]
        term = jnp.where(
            lane < GAP,
            -pltpu.roll(own, YL - GAP, 1),
            jnp.where(lane < 2 * GAP, pltpu.roll(own, GAP, 1), 0.0),
        )
        far = pltpu.roll(got_dh[level], YL + (GAP + nx - 1) - 2 * GAP, 1)
        term = term - jnp.where(lane == GAP + nx - 1, far, 0.0)
        return hy, hz, got_ye[level], got_yh[level] + scale * term

    loads[0].wait()
    loads[1].wait()
    prepare(0, e0, hp, hp)
    pl.semaphore_wait(barrier, len(peers))
    copies = send(0, e0)

    loads[2].wait()
    table = phase_table(tick)
    terms = [
        [jnp.broadcast_to(table[0:1, n * 8 + k : n * 8 + k + 1], (DZ, YL)) for k in range(8)]
        for n in range(STEPS)
    ]

    def weigh(x, carry):
        for c in range(3):
            sums = [None, None]
            for k in range(8):
                value = fwd[k * 3 + c, x].astype(F32)
                for n in range(STEPS):
                    part = terms[n][k] * value
                    sums[n] = part if sums[n] is None else sums[n] + part
            for n in range(STEPS):
                w[n, c, x, pl.ds(OFF, DZ)] = sums[n]
        return carry

    lax.fori_loop(0, nx, weigh, 0)
    loads[3].wait()
    loads[4].wait()
    for copy in copies:
        copy.wait()

    hy, hz, col_e, col_h = receive(0, e0, hp)
    col_e_out[...] = col_e
    col_h_out[...] = col_h

    def advance(x, prev):
        return e_update(
            x, prev, hp, e0, j0, mat, col_e_out[...], col_h_out[...], coef[0], coef[1], (e1, hp, j1)
        )

    lax.fori_loop(0, nx, advance, (hy, hz))
    prepare(1, e1, hp, h1)
    copies = send(1, e1)

    col_slab = got_ye[0, pl.ds(W0, WN)]

    def level_grad(x, carry):
        grad[x] = window_grad(x, e0, col_slab, w, 0)
        return carry

    lax.fori_loop(0, nx, level_grad, 0)
    for copy in copies:
        copy.wait()
    hy, hz, col_e, col_h = receive(1, e1, h1)
    rim_x[0] = hy
    rim_x[1] = hz
    col_e_out[...] = col_e
    col_h_out[...] = col_h


def finish_kernel(
    nx,
    e1, h1, j1, mat, w, grad, coef, rim_x, col_e, col_h,
    e_res, h_res, j_res, g_res,
    e2, h2, j2, g2, sem, g_sem,
):
    def copies(x):
        return [
            pltpu.make_async_copy(src.at[:, x], dst.at[:, x], sem.at[i, x])
            for i, (src, dst) in enumerate(((e2, e_res), (h2, h_res), (j2, j_res)))
        ]

    def advance(x, prev):
        out = e_update(
            x, prev, h1, e1, j1, mat, col_e[...], col_h[...], coef[0], coef[1], (e2, h2, j2)
        )
        for copy in copies(x):
            copy.start()
        return out

    def level_grad(x, carry):
        total = grad[x] + window_grad(x, e1, col_e[pl.ds(W0, WN)], w, 1)
        g2[x] = total[OFF : OFF + DZ]
        return carry

    lax.fori_loop(0, nx, advance, (rim_x[0], rim_x[1]))
    lax.fori_loop(0, nx, level_grad, 0)
    g_copy = pltpu.make_async_copy(g2, g_res, g_sem)
    g_copy.start()

    def drain(x, carry):
        for copy in copies(x):
            copy.wait()
        return carry

    lax.fori_loop(0, nx, drain, 0)
    g_copy.wait()


def body(gx, gy, e_field, h_field, current, material, pml_cells, forward_field, time_index):
    nx = e_field.shape[1]
    field = (3, nx, Z, YL)
    padded = (3, nx + 1, Z, YL)
    plane = (Z, YL)
    any_spec = pl.BlockSpec(memory_space=pl.ANY)
    smem = pl.BlockSpec(memory_space=pltpu.SMEM)
    vmem = pl.BlockSpec(memory_space=pltpu.VMEM)
    kept = [
        (padded, F32), (field, F32), (field, F32), ((nx, Z, YL), jnp.int32), ((STEPS, 3, nx, WN, YL), F32),
        ((nx, WN, YL), F32), ((2,) + plane, F32), ((2,) + plane, F32), (plane, F32), (plane, F32),
    ]
    mid = pl.pallas_call(
        functools.partial(exchange_kernel, gx, gy, nx),
        out_shape=[pltpu.VMEM(shape, dtype) for shape, dtype in kept],
        in_specs=[smem, smem] + [any_spec] * 5,
        out_specs=[vmem] * len(kept),
        scratch_shapes=[
            pltpu.VMEM(padded, F32),
            pltpu.VMEM(field, F32),
            pltpu.VMEM(field, F32),
            pltpu.VMEM(forward_field.shape, forward_field.dtype),
            pltpu.VMEM((STEPS,) + plane, F32),
            pltpu.VMEM((STEPS,) + plane, F32),
            pltpu.VMEM((STEPS, 2) + plane, F32),
            pltpu.VMEM((STEPS, 2) + plane, F32),
            pltpu.VMEM((STEPS, WN, YL), F32),
            pltpu.VMEM((STEPS, 2) + plane, F32),
            pltpu.VMEM((STEPS,) + plane, F32),
            pltpu.VMEM((STEPS,) + plane, F32),
            pltpu.VMEM((STEPS,) + plane, F32),
            pltpu.VMEM((STEPS,) + plane, F32),
            pltpu.SemaphoreType.DMA((5,)),
            pltpu.SemaphoreType.DMA((STEPS, 7)),
            pltpu.SemaphoreType.DMA((STEPS, 7)),
        ],
        compiler_params=pltpu.CompilerParams(
            collective_id=0, has_side_effects=True, vmem_limit_bytes=24 << 20
        ),
        name="exchange",
    )(pml_cells, time_index, e_field, h_field, current, material, forward_field)
    return pl.pallas_call(
        functools.partial(finish_kernel, nx),
        out_shape=[
            jax.ShapeDtypeStruct(field, F32),
            jax.ShapeDtypeStruct(field, F32),
            jax.ShapeDtypeStruct(field, F32),
            jax.ShapeDtypeStruct((nx, DZ, YL), F32),
        ],
        in_specs=[vmem] * len(kept),
        out_specs=[any_spec] * 4,
        scratch_shapes=[
            pltpu.VMEM(field, F32),
            pltpu.VMEM(field, F32),
            pltpu.VMEM(field, F32),
            pltpu.VMEM((nx, DZ, YL), F32),
            pltpu.SemaphoreType.DMA((3, nx)),
            pltpu.SemaphoreType.DMA(()),
        ],
        compiler_params=pltpu.CompilerParams(vmem_limit_bytes=24 << 20),
        name="finish",
    )(*mid)


def solution(mesh):
    field = P(None, "gx", None, "gy")
    cell = P("gx", None, "gy")
    return jax.shard_map(
        functools.partial(body, mesh.shape["gx"], mesh.shape["gy"]),
        mesh=mesh,
        in_specs=(field, field, field, cell, P(), field, P()),
        out_specs=(field, field, field, cell),
        check_vma=False,
    )
```

time: 104 us -> 36.2 us (0.35)
  the two profiles are of different devices: /device:TPU:8 before, /device:TPU:1 now
where the time goes in v1:
time: 36.2 us; the launch traced here: 36 us
  Pallas kernels  30.1 us (83%)
  local copies, waits for them, and re-layouts  4.62 us (13%)
  between operations  1.34 us (4%)
    pallas_call x1, Pallas kernels, body(): pl.pallas_call(functools.partial(exchange_kernel, gx, gy, nx), out_shape=...  25.5 us
    pallas_call x1, Pallas kernels, body(): pl.pallas_call(functools.partial(finish_kernel, nx), out_shape=[jax.Shape...  4.6 us
    unnamed x11, local copies, waits for them, and re-layouts  3.95 us

profile of v1, /device:TPU:1, one launch (start us, length us, event | category | flops | bytes accessed | tf_op | source)
XLA Modules:
  0.0 36.0 jit_solution(15334940166129369209)
XLA Ops:
  1.3 0.0 copy-start
  1.3 0.0 copy-start.1
  1.3 0.0 copy-start.3
  1.3 1.8 %copy.11.f_in = bf16[24,16,12,128]{3,2,1,0:T(8,128)(2,1)S(1)} copy(bf16[24,16,12,128]{3,1,2,0:T(8,128)(2,1)} %param.12) | data formatting | bytes 2359296 | tf_op args[5]
  3.1 0.0 copy-done
  3.1 0.1 copy-done.1
  3.3 0.1 copy-done.3
  3.3 0.0 copy-start.2
  3.3 1.3 %copy-done.2 = f32[3,16,48,128]{3,2,1,0:T(8,128)S(1)} copy-done((f32[3,16,48,128]{3,2,1,0:T(8,128)S(1)}, f32[3,16,48,128]{3,2,1,0:T(8,128)}, u32[]{:S(2)}) %copy-start.2) | copy-done | bytes 1179672
  4.6 0.0 copy-start.4
  4.6 0.7 %copy-done.4 = s32[2]{0:T(128)S(1)} copy-done((s32[2]{0:T(128)S(1)}, s32[2]{0:T(128)}, u32[]{:S(2)}) %copy-start.4) | copy-done | bytes 32
  5.3 25.5 %exchange.1 = (f32[3,17,48,128]{3,2,1,0:T(8,128)S(1)}, f32[3,16,48,128]{3,2,1,0:T(8,128)S(1)}, f32[3,16,48,128]{3,2,1,0:T(8,128)S(1)}, s32[16,48,128]{2,1,0:T(8,...) custom-call(s32[2]{0:T(128)S(1)} %copy-done.4, ...), custom_call_target="tpu_custom_call" | custom-call | tf_op jit(solution)/shard_map/exchange/pallas_call | solution.py:350
  30.7 4.6 %finish.1 = (f32[3,16,48,128]{3,2,1,0:T(8,128)}, f32[3,16,48,128]{3,2,1,0:T(8,128)}, f32[3,16,48,128]{3,2,1,0:T(8,128)}, f32[16,12,128]{2,1,0:T(8,128)S(1)}) custom-call(f32[3,17,48,128]{3,2,1,0:T(8,128)S(1)} %get-tuple-element.14.e1, f32[3,16,48,128]{3,2,1,0:T(8,128)S(1)} %get-tuple-element.15.h1, f32[3,16,48,128]{3,2,1,0:T(8,128)S(1)} %get-tuple-element.16.j1, ...), custom_call_target="tpu_custom_call" | custom-call | tf_op jit(solution)/shard_map/finish/pallas_call | solution.py:379
  35.3 0.7 %copy.12 = f32[16,12,128]{2,0,1:T(8,128)} copy(f32[16,12,128]{2,1,0:T(8,128)S(1)} %get-tuple-element.27) | data formatting | bytes 196608 | tf_op jit(solution)/shard_map/finish/pallas_call | solution.py:379
Async XLA Ops:
  1.3 1.9 %copy-start = (f32[3,16,48,128]{3,2,1,0:T(8,128)S(1)}, f32[3,16,48,128]{3,2,1,0:T(8,128)}, u32[]{:S(2)}) copy-start(f32[3,16,48,128]{3,2,1,0:T(8,128)} %e_in.1) | copy-start | bytes 3538948
  1.3 2.0 %copy-start.1 = (f32[3,16,48,128]{3,2,1,0:T(8,128)S(1)}, f32[3,16,48,128]{3,2,1,0:T(8,128)}, u32[]{:S(2)}) copy-start(f32[3,16,48,128]{3,2,1,0:T(8,128)} %h_in.1) | copy-start | bytes 3538948
  1.3 2.0 %copy-start.3 = (s32[16,48,128]{2,1,0:T(8,128)S(1)}, s32[16,48,128]{2,1,0:T(8,128)}, u32[]{:S(2)}) copy-start(s32[16,48,128]{2,1,0:T(8,128)} %m_in.1) | copy-start | bytes 1179652
  3.3 1.3 %copy-start.2 = (f32[3,16,48,128]{3,2,1,0:T(8,128)S(1)}, f32[3,16,48,128]{3,2,1,0:T(8,128)}, u32[]{:S(2)}) copy-start(f32[3,16,48,128]{3,2,1,0:T(8,128)} %j_in.1) | copy-start | bytes 3538948
  4.6 0.7 %copy-start.4 = (s32[2]{0:T(128)S(1)}, s32[2]{0:T(128)}, u32[]{:S(2)}) copy-start(s32[2]{0:T(128)} %pml.1) | copy-start | bytes 28

commit v2 on v1

v2 whole, which is shorter than its diff:
```python
import functools
import math

import jax
import jax.numpy as jnp
from jax import lax
from jax.experimental import pallas as pl
from jax.experimental.pallas import tpu as pltpu
from jax.sharding import PartitionSpec as P

Z = 48
DZ = 12
FREQ = 4
STEPS = 2
Z0 = 18
W0 = 16
WN = 16
YL = 128
CHUNKS = 4
GAP = 16

COURANT = 0.5
SIGMA_PEAK = 0.8
DRUDE_KEEP = 0.95 / 1.05
DRUDE_GAIN = 0.25 / 1.05
PERIOD_STEPS = 64
F32 = jnp.float32
MESH = pl.DeviceIdType.MESH


def lanes():
    return lax.broadcasted_iota(jnp.int32, (Z, YL), 1)


def rows():
    return lax.broadcasted_iota(jnp.int32, (Z, YL), 0)


def z_next(v):
    return jnp.where(rows() == Z - 1, 0.0, pltpu.roll(v, Z - 1, 0))


def z_prev(v):
    return jnp.where(rows() == 0, 0.0, pltpu.roll(v, 1, 0))


def absorber(pml):
    low = pml[0]
    high = pml[1]
    z = rows()
    low_depth = jnp.maximum(low - z, 0).astype(F32) / low.astype(F32)
    high_depth = jnp.maximum(z - (Z - 1 - high), 0).astype(F32) / high.astype(F32)
    sigma = SIGMA_PEAK * (low_depth * low_depth * low_depth + high_depth * high_depth * high_depth)
    half_loss = 1.0 + 0.5 * sigma
    return (1.0 - 0.5 * sigma) / half_loss, COURANT / half_loss


def phase_table(tick):
    lane = lax.broadcasted_iota(jnp.int32, (8, YL), 1)
    level = lane // 8
    freq = (lane % 8) // 2
    turn = ((3 + freq) * (tick[0] - level)) & (PERIOD_STEPS - 1)
    angle = turn.astype(F32) * (2.0 * math.pi / PERIOD_STEPS)
    return jnp.where(lane % 2 == 0, jnp.cos(angle), -jnp.sin(angle))


def h_partial(x, e, h, h_out, decay, scale, packs):
    lane = lanes()
    ex, ey, ez = e[0, x], e[1, x], e[2, x]
    last = lane == YL - 1
    ez_yn = jnp.where(last, 0.0, pltpu.roll(ez, YL - 1, 1))
    ex_yn = jnp.where(last, 0.0, pltpu.roll(ex, YL - 1, 1))
    hx = decay * h[0, x] - scale * (ez_yn - ez - (z_next(ey) - ey))
    hy = decay * h[1, x] - scale * (z_next(ex) - ex - (e[2, x + 1] - ez))
    hz = decay * h[2, x] - scale * (e[1, x + 1] - ey - (ex_yn - ex))
    h_out[0, x] = hx
    h_out[1, x] = hy
    h_out[2, x] = hz
    first_cols, last_cols = packs
    for group, v in enumerate((ex, ez, ey)):
        at = GAP * group + x
        first_cols = jnp.where(lane == at, pltpu.roll(v, at, 1), first_cols)
    for group, v in enumerate((hx, hz)):
        at = GAP * group + x
        last_cols = jnp.where(lane == at, pltpu.roll(v, at + 1, 1), last_cols)
    return first_cols, last_cols


def column_to_tile(column):
    row = jnp.sum(jnp.where(lanes() == rows(), column, 0.0), axis=0, keepdims=True)
    return jnp.broadcast_to(row, (8, YL))


def tile_to_column(tile):
    return jnp.sum(jnp.where(lanes() == rows(), tile[0:1], 0.0), axis=1, keepdims=True)


def h_full(x, hp, col_e, scale):
    last = lanes() == YL - 1
    ex_halo = pltpu.roll(col_e, YL - 1 - x, 1)
    ez_halo = pltpu.roll(col_e, YL - 1 - GAP - x, 1)
    hx = hp[0, x] - jnp.where(last, scale * ez_halo, 0.0)
    hz = hp[2, x] + jnp.where(last, scale * ex_halo, 0.0)
    return hx, hp[1, x], hz


def e_update(x, prev, hp, e, j, mat, col_e, col_h, decay, scale, outs):
    lane = lanes()
    e_out, h_out, j_out = outs
    hy_xp, hz_xp = prev
    first = lane == 0
    hx, hy, hz = h_full(x, hp, col_e, scale)
    h_out[0, x] = hx
    h_out[1, x] = hy
    h_out[2, x] = hz
    hx_yp = jnp.where(first, pltpu.roll(col_h, YL - x, 1), pltpu.roll(hx, 1, 1))
    hz_yp = jnp.where(first, pltpu.roll(col_h, YL - GAP - x, 1), pltpu.roll(hz, 1, 1))
    m = mat[x]
    metal = m == 2
    e_scale = scale * jnp.where(m == 1, 0.25, 1.0)
    backs = (
        hz - hz_yp - (hy - z_prev(hy)),
        hx - z_prev(hx) - (hz - hz_xp),
        hy - hy_xp - (hx - hx_yp),
    )
    for c, back in enumerate(backs):
        j_now = j[c, x]
        e_new = decay * e[c, x] + e_scale * (back - jnp.where(metal, j_now, 0.0))
        e_out[c, x] = e_new
        j_out[c, x] = jnp.where(metal, DRUDE_KEEP * j_now + DRUDE_GAIN * e_new, 0.0)
    return hy, hz


def slab_grad(z, e, col_e, w, level):
    nx = e.shape[1] - 1
    lane = lax.broadcasted_iota(jnp.int32, (nx, YL), 1)
    sub = lax.broadcasted_iota(jnp.int32, (nx, YL), 0)

    def cells(c, x, k):
        return e[c, pl.ds(x, nx), k]

    k = Z0 + z
    ex, ey, ez = cells(0, 0, k), cells(1, 0, k), cells(2, 0, k)
    ex_xn, ez_zn = cells(0, 1, k), cells(2, 0, k + 1)
    halo = jnp.sum(jnp.where(lane == 2 * GAP + sub, col_e[k : k + 1], 0.0), axis=1, keepdims=True)
    ey_yn = jnp.where(lane == YL - 1, halo, pltpu.roll(ey, YL - 1, 1))
    return 0.5 * (
        (ex + ex_xn) * w[level, 0, z] + (ey + ey_yn) * w[level, 1, z] + (ez + ez_zn) * w[level, 2, z]
    )


def exchange_kernel(
    gx, gy, nx,
    pml_in, tick_in, e_in, h_in, j_in, m_in, f_in,
    e1, h1, j1, mat, w, grad, coef, rim_x, col_e_out, col_h_out,
    pml, tick, e0, hp, j0, fwd, pack_e, pack_h, send_h, tile_e, tile_h,
    got_e, got_slab, got_h, got_ye, got_yh, got_de, got_dh,
    field_sem, load_sem, send_sem, recv_sem,
):
    me_x = lax.axis_index("gx")
    me_y = lax.axis_index("gy")
    x_next, x_prev = lax.rem(me_x + 1, gx), lax.rem(me_x + gx - 1, gx)
    y_next, y_prev = lax.rem(me_y + 1, gy), lax.rem(me_y + gy - 1, gy)
    barrier = pltpu.get_barrier_semaphore()
    peers = (
        (x_prev, me_y), (x_next, me_y), (me_x, y_prev), (me_x, y_next), (x_next, y_prev), (x_prev, y_next),
    )
    for peer in peers:
        pl.semaphore_signal(barrier, inc=1, device_id=peer, device_id_type=MESH)

    small = [
        pltpu.make_async_copy(pml_in, pml, load_sem.at[3]),
        pltpu.make_async_copy(tick_in, tick, load_sem.at[4]),
    ]
    fields = []
    for i in reversed(range(CHUNKS)):
        span = pl.ds(i * nx // CHUNKS, nx // CHUNKS)
        fields.append(
            [
                pltpu.make_async_copy(e_in.at[:, span], e0.at[:, span], field_sem.at[0, i]),
                pltpu.make_async_copy(h_in.at[:, span], hp.at[:, span], field_sem.at[1, i]),
            ]
        )
    late = [
        pltpu.make_async_copy(f_in, fwd, load_sem.at[0]),
        pltpu.make_async_copy(j_in, j0, load_sem.at[1]),
        pltpu.make_async_copy(m_in, mat, load_sem.at[2]),
    ]
    for load in small + sum(fields, []) + late:
        load.start()
    for load in small:
        load.wait()

    lane = lanes()
    decay, scale = absorber(pml)
    coef[0] = decay
    coef[1] = scale
    zero = jnp.zeros((Z, YL), F32)
    for c in range(3):
        e0[c, nx] = zero
        e1[c, nx] = zero

    def route(level, i, e):
        src, dst, peer = (
            (e.at[pl.ds(1, 2), 0], got_e, 0),
            (e.at[0, 0, pl.ds(W0, WN)], got_slab, 0),
            (send_h.at[level], got_h, 1),
            (pack_e.at[level], got_ye, 2),
            (pack_h.at[level], got_yh, 3),
            (tile_e.at[level], got_de, 4),
            (tile_h.at[level], got_dh, 5),
        )[i]
        return pltpu.make_async_remote_copy(
            src_ref=src,
            dst_ref=dst.at[level],
            send_sem=send_sem.at[level, i],
            recv_sem=recv_sem.at[level, i],
            device_id=peers[peer],
            device_id_type=MESH,
        )

    def send(level, e, which):
        copies = [route(level, i, e) for i in which]
        for copy in copies:
            copy.start()
        return copies

    def last_plane(level, e, h, h_out):
        packs = h_partial(nx - 1, e, h, h_out, coef[0], coef[1], (zero, zero))
        send_h[level, 0] = h_out[1, nx - 1]
        send_h[level, 1] = h_out[2, nx - 1]
        tile_h[level] = column_to_tile(e[1, 0, :, YL - 1 : YL])
        tile_e[level] = column_to_tile(e[0, nx - 1, :, 0:1])
        return packs

    def receive(level, e, h):
        e[0, nx, pl.ds(W0, WN)] = got_slab[level]
        h[1, nx - 1] = h[1, nx - 1] + scale * got_e[level, 1]
        h[2, nx - 1] = h[2, nx - 1] - scale * got_e[level, 0]
        corner = jnp.where(lane == YL - 1, tile_to_column(got_de[level]), 0.0)
        hy = got_h[level, 0] + scale * e[2, 0]
        hz = got_h[level, 1] + scale * (corner - e[1, 0])
        own = pack_e[level]
        term = jnp.where(
            lane < GAP,
            -pltpu.roll(own, YL - GAP, 1),
            jnp.where(lane < 2 * GAP, pltpu.roll(own, GAP, 1), 0.0),
        )
        term = term - jnp.where(lane == GAP + nx - 1, tile_to_column(got_dh[level]), 0.0)
        return hy, hz, got_ye[level], got_yh[level] + scale * term

    def plane(step, packs, e, h, h_out):
        return h_partial(nx - 2 - step, e, h, h_out, coef[0], coef[1], packs)

    packs = None
    for i, parts in enumerate(fields):
        for load in parts:
            load.wait()
        if i == 0:
            head = functools.partial(h_partial, nx - 1, e0, hp, hp, decay, scale)
            packs = head((zero, zero))
        size = nx // CHUNKS
        packs = lax.fori_loop(
            max(i * size - 1, 0),
            (i + 1) * size - 1,
            functools.partial(plane, e=e0, h=hp, h_out=hp),
            packs,
        )
    pack_e[0] = packs[0]
    pack_h[0] = packs[1]
    send_h[0, 0] = hp[1, nx - 1]
    send_h[0, 1] = hp[2, nx - 1]
    tile_h[0] = column_to_tile(e0[1, 0, :, YL - 1 : YL])
    tile_e[0] = column_to_tile(e0[0, nx - 1, :, 0:1])
    pl.semaphore_wait(barrier, len(peers))
    copies = send(0, e0, (5, 4, 3, 2, 0, 1, 6))

    late[0].wait()
    table = phase_table(tick)
    terms = [
        [jnp.broadcast_to(table[0:1, n * 8 + k : n * 8 + k + 1], (nx, YL)) for k in range(8)]
        for n in range(STEPS)
    ]

    def weigh(z, carry):
        for c in range(3):
            sums = [None, None]
            for k in range(8):
                value = fwd[k * 3 + c, z].astype(F32)
                for n in range(STEPS):
                    part = terms[n][k] * value
                    sums[n] = part if sums[n] is None else sums[n] + part
            for n in range(STEPS):
                w[n, c, z] = sums[n]
        return carry

    lax.fori_loop(0, DZ, weigh, 0)
    late[1].wait()
    late[2].wait()
    for copy in copies:
        copy.wait()

    hy, hz, col_e, col_h = receive(0, e0, hp)
    col_e_out[...] = col_e
    col_h_out[...] = col_h

    def advance(x, prev):
        return e_update(
            x, prev, hp, e0, j0, mat, col_e_out[...], col_h_out[...], coef[0], coef[1], (e1, hp, j1)
        )

    prev = advance(0, (hy, hz))
    copies = send(1, e1, (0, 1))
    advance(nx - 1, h_full(nx - 2, hp, col_e_out[...], coef[1])[1:])
    packs = last_plane(1, e1, hp, h1)
    copies += send(1, e1, (2, 5, 6))
    lax.fori_loop(1, nx - 1, advance, prev)
    packs = lax.fori_loop(0, nx - 1, functools.partial(plane, e=e1, h=hp, h_out=h1), packs)
    pack_e[1] = packs[0]
    pack_h[1] = packs[1]
    copies += send(1, e1, (3, 4))

    for z in range(DZ):
        grad[z] = slab_grad(z, e0, got_ye.at[0], w, 0)
    for copy in copies:
        copy.wait()
    hy, hz, col_e, col_h = receive(1, e1, h1)
    rim_x[0] = hy
    rim_x[1] = hz
    col_e_out[...] = col_e
    col_h_out[...] = col_h


def finish_kernel(
    nx,
    e1, h1, j1, mat, w, grad, coef, rim_x, col_e, col_h,
    e_res, h_res, j_res, g_res,
    e2, h2, j2, g2, sem, g_sem,
):
    def copies(x):
        return [
            pltpu.make_async_copy(src.at[:, x], dst.at[:, x], sem.at[i, x])
            for i, (src, dst) in enumerate(((e2, e_res), (h2, h_res), (j2, j_res)))
        ]

    def advance(x, prev):
        out = e_update(
            x, prev, h1, e1, j1, mat, col_e[...], col_h[...], coef[0], coef[1], (e2, h2, j2)
        )
        for copy in copies(x):
            copy.start()
        return out

    lax.fori_loop(0, nx, advance, (rim_x[0], rim_x[1]))
    for z in range(DZ):
        g2[z] = grad[z] + slab_grad(z, e1, col_e, w, 1)
    g_copy = pltpu.make_async_copy(g2, g_res, g_sem)
    g_copy.start()

    def drain(x, carry):
        for copy in copies(x):
            copy.wait()
        return carry

    lax.fori_loop(0, nx, drain, 0)
    g_copy.wait()


def body(gx, gy, e_field, h_field, current, material, pml_cells, forward_field, time_index):
    nx = e_field.shape[1]
    slab = jnp.transpose(forward_field, (0, 2, 1, 3))
    field = (3, nx, Z, YL)
    padded = (3, nx + 1, Z, YL)
    plane = (Z, YL)
    any_spec = pl.BlockSpec(memory_space=pl.ANY)
    hbm = pl.BlockSpec(memory_space=pltpu.HBM)
    vmem = pl.BlockSpec(memory_space=pltpu.VMEM)
    kept = [
        (padded, F32), (field, F32), (field, F32), ((nx, Z, YL), jnp.int32), ((STEPS, 3, DZ, nx, YL), F32),
        ((DZ, nx, YL), F32), ((2,) + plane, F32), ((2,) + plane, F32), (plane, F32), (plane, F32),
    ]
    mid = pl.pallas_call(
        functools.partial(exchange_kernel, gx, gy, nx),
        out_shape=[pltpu.VMEM(shape, dtype) for shape, dtype in kept],
        in_specs=[hbm] * 7,
        out_specs=[vmem] * len(kept),
        scratch_shapes=[
            pltpu.SMEM((2,), jnp.int32),
            pltpu.SMEM((1,), jnp.int32),
            pltpu.VMEM(padded, F32),
            pltpu.VMEM(field, F32),
            pltpu.VMEM(field, F32),
            pltpu.VMEM(slab.shape, slab.dtype),
            pltpu.VMEM((STEPS,) + plane, F32),
            pltpu.VMEM((STEPS,) + plane, F32),
            pltpu.VMEM((STEPS, 2) + plane, F32),
            pltpu.VMEM((STEPS, 8, YL), F32),
            pltpu.VMEM((STEPS, 8, YL), F32),
            pltpu.VMEM((STEPS, 2) + plane, F32),
            pltpu.VMEM((STEPS, WN, YL), F32),
            pltpu.VMEM((STEPS, 2) + plane, F32),
            pltpu.VMEM((STEPS,) + plane, F32),
            pltpu.VMEM((STEPS,) + plane, F32),
            pltpu.VMEM((STEPS, 8, YL), F32),
            pltpu.VMEM((STEPS, 8, YL), F32),
            pltpu.SemaphoreType.DMA((2, CHUNKS)),
            pltpu.SemaphoreType.DMA((5,)),
            pltpu.SemaphoreType.DMA((STEPS, 7)),
            pltpu.SemaphoreType.DMA((STEPS, 7)),
        ],
        compiler_params=pltpu.CompilerParams(
            collective_id=0, has_side_effects=True, vmem_limit_bytes=58 << 20
        ),
        name="exchange",
    )(pml_cells, time_index, e_field, h_field, current, material, slab)
    e, h, j, grad = pl.pallas_call(
        functools.partial(finish_kernel, nx),
        out_shape=[
            jax.ShapeDtypeStruct(field, F32),
            jax.ShapeDtypeStruct(field, F32),
            jax.ShapeDtypeStruct(field, F32),
            jax.ShapeDtypeStruct((DZ, nx, YL), F32),
        ],
        in_specs=[vmem] * len(kept),
        out_specs=[any_spec] * 4,
        scratch_shapes=[
            pltpu.VMEM(field, F32),
            pltpu.VMEM(field, F32),
            pltpu.VMEM(field, F32),
            pltpu.VMEM((DZ, nx, YL), F32),
            pltpu.SemaphoreType.DMA((3, nx)),
            pltpu.SemaphoreType.DMA(()),
        ],
        compiler_params=pltpu.CompilerParams(vmem_limit_bytes=24 << 20),
        name="finish",
    )(*mid)
    return e, h, j, jnp.transpose(grad, (1, 0, 2))


def solution(mesh):
    field = P(None, "gx", None, "gy")
    cell = P("gx", None, "gy")
    return jax.shard_map(
        functools.partial(body, mesh.shape["gx"], mesh.shape["gy"]),
        mesh=mesh,
        in_specs=(field, field, field, cell, P(), field, P()),
        out_specs=(field, field, field, cell),
        check_vma=False,
    )
```

time: 36.2 us -> 28.7 us (0.79)
  the two profiles are of different devices: /device:TPU:1 before, /device:TPU:8 now
where the time goes in v2:
time: 28.7 us; the launch traced here: 28.6 us
  Pallas kernels  27.3 us (95%)
  between operations  1.29 us (4%)
    pallas_call x1, Pallas kernels, body(): pl.pallas_call(functools.partial(exchange_kernel, gx, gy, nx), out_shape=...  23.2 us
    pallas_call x1, Pallas kernels, body(): pl.pallas_call(functools.partial(finish_kernel, nx), out_shape=[jax.Shape...  4.06 us

profile of v2, /device:TPU:8, one launch (start us, length us, event | category | flops | bytes accessed | tf_op | source)
XLA Modules:
  0.0 28.6 jit_solution(6017577089320695051)
XLA Ops:
  1.3 23.2 %exchange.1 = (f32[3,17,48,128]{3,2,1,0:T(8,128)S(1)}, f32[3,16,48,128]{3,2,1,0:T(8,128)S(1)}, f32[3,16,48,128]{3,2,1,0:T(8,128)S(1)}, s32[16,48,128]{2,1,0:T(8,...) custom-call(s32[2]{0:T(128)} %pml_in.1, ...), custom_call_target="tpu_custom_call" | custom-call | tf_op jit(solution)/shard_map/exchange/pallas_call | solution.py:382
  24.5 4.1 %finish.1 = (f32[3,16,48,128]{3,2,1,0:T(8,128)}, f32[3,16,48,128]{3,2,1,0:T(8,128)}, f32[3,16,48,128]{3,2,1,0:T(8,128)}, f32[12,16,128]{2,1,0:T(8,128)}) custom-call(f32[3,17,48,128]{3,2,1,0:T(8,128)S(1)} %get-tuple-element.18.e1, f32[3,16,48,128]{3,2,1,0:T(8,128)S(1)} %get-tuple-element.19.h1, f32[3,16,48,128]{3,2,1,0:T(8,128)S(1)} %get-tuple-element.20.j1, ...), custom_call_target="tpu_custom_call" | custom-call | tf_op jit(solution)/shard_map/finish/pallas_call | solution.py:416

commit v3 on v2

--- a/solution.py
+++ b/solution.py
@@ -152,7 +152,7 @@
 def exchange_kernel(
     gx, gy, nx,
     pml_in, tick_in, e_in, h_in, j_in, m_in, f_in,
-    e1, h1, j1, mat, w, grad, coef, rim_x, col_e_out, col_h_out,
+    e1, h1, j1, e2, mat, w, grad, coef, rim_x, col_e_out, col_h_out,
     pml, tick, e0, hp, j0, fwd, pack_e, pack_h, send_h, tile_e, tile_h,
     got_e, got_slab, got_h, got_ye, got_yh, got_de, got_dh,
     field_sem, load_sem, send_sem, recv_sem,
@@ -225,29 +225,33 @@
             copy.start()
         return copies
 
-    def last_plane(level, e, h, h_out):
-        packs = h_partial(nx - 1, e, h, h_out, coef[0], coef[1], (zero, zero))
-        send_h[level, 0] = h_out[1, nx - 1]
-        send_h[level, 1] = h_out[2, nx - 1]
+    def pack(level, e, h, packs):
+        pack_e[level] = packs[0]
+        pack_h[level] = packs[1]
+        send_h[level, 0] = h[1, nx - 1]
+        send_h[level, 1] = h[2, nx - 1]
         tile_h[level] = column_to_tile(e[1, 0, :, YL - 1 : YL])
         tile_e[level] = column_to_tile(e[0, nx - 1, :, 0:1])
-        return packs
 
     def receive(level, e, h):
         e[0, nx, pl.ds(W0, WN)] = got_slab[level]
         h[1, nx - 1] = h[1, nx - 1] + scale * got_e[level, 1]
         h[2, nx - 1] = h[2, nx - 1] - scale * got_e[level, 0]
-        corner = jnp.where(lane == YL - 1, tile_to_column(got_de[level]), 0.0)
-        hy = got_h[level, 0] + scale * e[2, 0]
-        hz = got_h[level, 1] + scale * (corner - e[1, 0])
         own = pack_e[level]
         term = jnp.where(
             lane < GAP,
             -pltpu.roll(own, YL - GAP, 1),
             jnp.where(lane < 2 * GAP, pltpu.roll(own, GAP, 1), 0.0),
         )
-        term = term - jnp.where(lane == GAP + nx - 1, tile_to_column(got_dh[level]), 0.0)
-        return hy, hz, got_ye[level], got_yh[level] + scale * term
+        col_e_out[...] = got_ye[level]
+        col_h_out[...] = got_yh[level] + scale * term
+
+    def receive_corners(level, e):
+        far = tile_to_column(got_dh[level])
+        col_h_out[...] = col_h_out[...] - jnp.where(lane == GAP + nx - 1, scale * far, 0.0)
+        corner = jnp.where(lane == YL - 1, tile_to_column(got_de[level]), 0.0)
+        rim_x[0] = got_h[level, 0] + scale * e[2, 0]
+        rim_x[1] = got_h[level, 1] + scale * (corner - e[1, 0])
 
     def plane(step, packs, e, h, h_out):
         return h_partial(nx - 2 - step, e, h, h_out, coef[0], coef[1], packs)
@@ -266,14 +270,10 @@
             functools.partial(plane, e=e0, h=hp, h_out=hp),
             packs,
         )
-    pack_e[0] = packs[0]
-    pack_h[0] = packs[1]
-    send_h[0, 0] = hp[1, nx - 1]
-    send_h[0, 1] = hp[2, nx - 1]
-    tile_h[0] = column_to_tile(e0[1, 0, :, YL - 1 : YL])
-    tile_e[0] = column_to_tile(e0[0, nx - 1, :, 0:1])
+    pack(0, e0, hp, packs)
     pl.semaphore_wait(barrier, len(peers))
-    copies = send(0, e0, (5, 4, 3, 2, 0, 1, 6))
+    corners = send(0, e0, (5, 6))
+    copies = send(0, e0, (4, 3, 2, 0, 1))
 
     late[0].wait()
     table = phase_table(tick)
@@ -300,70 +300,72 @@
     for copy in copies:
         copy.wait()
 
-    hy, hz, col_e, col_h = receive(0, e0, hp)
-    col_e_out[...] = col_e
-    col_h_out[...] = col_h
-
-    def advance(x, prev):
+    receive(0, e0, hp)
+
+    def advance(x, prev, e, h, j, e_next, j_next):
         return e_update(
-            x, prev, hp, e0, j0, mat, col_e_out[...], col_h_out[...], coef[0], coef[1], (e1, hp, j1)
-        )
-
-    prev = advance(0, (hy, hz))
+            x, prev, h, e, j, mat, col_e_out[...], col_h_out[...], coef[0], coef[1], (e_next, h, j_next)
+        )
+
+    first = functools.partial(advance, e=e0, h=hp, j=j0, e_next=e1, j_next=j1)
+    second = functools.partial(advance, e=e1, h=h1, j=j1, e_next=e2, j_next=j1)
+
+    def inner(step, h):
+        return lax.fori_loop(1, nx - 1, step, h_full(0, h, col_e_out[...], coef[1])[1:])
+
+    prev = inner(first, hp)
+    packs = lax.fori_loop(1, nx - 2, functools.partial(plane, e=e1, h=hp, h_out=h1), (zero, zero))
+    for copy in corners:
+        copy.wait()
+    receive_corners(0, e0)
+    first(0, (rim_x[0], rim_x[1]))
     copies = send(1, e1, (0, 1))
-    advance(nx - 1, h_full(nx - 2, hp, col_e_out[...], coef[1])[1:])
-    packs = last_plane(1, e1, hp, h1)
-    copies += send(1, e1, (2, 5, 6))
-    lax.fori_loop(1, nx - 1, advance, prev)
-    packs = lax.fori_loop(0, nx - 1, functools.partial(plane, e=e1, h=hp, h_out=h1), packs)
-    pack_e[1] = packs[0]
-    pack_h[1] = packs[1]
-    copies += send(1, e1, (3, 4))
+    first(nx - 1, prev)
+    for x in (nx - 1, nx - 2, 0):
+        packs = h_partial(x, e1, hp, h1, coef[0], coef[1], packs)
+    pack(1, e1, h1, packs)
+    corners = send(1, e1, (5, 6))
+    copies += send(1, e1, (4, 3, 2))
 
     for z in range(DZ):
         grad[z] = slab_grad(z, e0, got_ye.at[0], w, 0)
     for copy in copies:
         copy.wait()
-    hy, hz, col_e, col_h = receive(1, e1, h1)
-    rim_x[0] = hy
-    rim_x[1] = hz
-    col_e_out[...] = col_e
-    col_h_out[...] = col_h
+    receive(1, e1, h1)
+    inner(second, h1)
+    for copy in corners:
+        copy.wait()
+    receive_corners(1, e1)
 
 
 def finish_kernel(
     nx,
-    e1, h1, j1, mat, w, grad, coef, rim_x, col_e, col_h,
+    e1, h1, j1, e2, mat, w, grad, coef, rim_x, col_e, col_h,
     e_res, h_res, j_res, g_res,
-    e2, h2, j2, g2, sem, g_sem,
+    e_rim, h_rim, j_rim, g2, sem, g_sem,
 ):
-    def copies(x):
-        return [
-            pltpu.make_async_copy(src.at[:, x], dst.at[:, x], sem.at[i, x])
-            for i, (src, dst) in enumerate(((e2, e_res), (h2, h_res), (j2, j_res)))
-        ]
-
-    def advance(x, prev):
-        out = e_update(
-            x, prev, h1, e1, j1, mat, col_e[...], col_h[...], coef[0], coef[1], (e2, h2, j2)
-        )
-        for copy in copies(x):
-            copy.start()
-        return out
-
-    lax.fori_loop(0, nx, advance, (rim_x[0], rim_x[1]))
+    fields = ((e2, e_rim, e_res), (h1, h_rim, h_res), (j1, j_rim, j_res))
+    mid = pl.ds(1, nx - 2)
+    copies = [
+        pltpu.make_async_copy(src.at[:, mid], dst.at[:, mid], sem.at[i, 0])
+        for i, (src, _, dst) in enumerate(fields)
+    ]
+    for copy in copies:
+        copy.start()
+    last = nx - 1
+    for n, x, prev in ((1, 0, (rim_x[0], rim_x[1])), (2, last, (h1[1, last - 1], h1[2, last - 1]))):
+        e_update(
+            x, prev, h1, e1, j1, mat, col_e[...], col_h[...], coef[0], coef[1], (e_rim, h_rim, j_rim)
+        )
+        for i, (_, src, dst) in enumerate(fields):
+            copies.append(pltpu.make_async_copy(src.at[:, x], dst.at[:, x], sem.at[i, n]))
+            copies[-1].start()
     for z in range(DZ):
         g2[z] = grad[z] + slab_grad(z, e1, col_e, w, 1)
-    g_copy = pltpu.make_async_copy(g2, g_res, g_sem)
-    g_copy.start()
-
-    def drain(x, carry):
-        for copy in copies(x):
-            copy.wait()
-        return carry
-
-    lax.fori_loop(0, nx, drain, 0)
-    g_copy.wait()
+    copies.append(pltpu.make_async_copy(g2, g_res, g_sem))
+    copies[-1].start()
+    for copy in copies:
+        copy.wait()
 
 
 def body(gx, gy, e_field, h_field, current, material, pml_cells, forward_field, time_index):
@@ -376,7 +378,7 @@
     hbm = pl.BlockSpec(memory_space=pltpu.HBM)
     vmem = pl.BlockSpec(memory_space=pltpu.VMEM)
     kept = [
-        (padded, F32), (field, F32), (field, F32), ((nx, Z, YL), jnp.int32), ((STEPS, 3, DZ, nx, YL), F32),
+        (padded, F32), (field, F32), (field, F32), (field, F32), ((nx, Z, YL), jnp.int32), ((STEPS, 3, DZ, nx, YL), F32),
         ((DZ, nx, YL), F32), ((2,) + plane, F32), ((2,) + plane, F32), (plane, F32), (plane, F32),
     ]
     mid = pl.pallas_call(
@@ -409,7 +411,7 @@
             pltpu.SemaphoreType.DMA((STEPS, 7)),
         ],
         compiler_params=pltpu.CompilerParams(
-            collective_id=0, has_side_effects=True, vmem_limit_bytes=58 << 20
+            collective_id=0, has_side_effects=True, vmem_limit_bytes=57 << 20
         ),
         name="exchange",
     )(pml_cells, time_index, e_field, h_field, current, material, slab)
@@ -428,7 +430,7 @@
             pltpu.VMEM(field, F32),
             pltpu.VMEM(field, F32),
             pltpu.VMEM((DZ, nx, YL), F32),
-            pltpu.SemaphoreType.DMA((3, nx)),
+            pltpu.SemaphoreType.DMA((3, 3)),
             pltpu.SemaphoreType.DMA(()),
         ],
         compiler_params=pltpu.CompilerParams(vmem_limit_bytes=24 << 20),

time: 28.7 us -> 29.5 us (1.028)
  Pallas kernels: 27.3 us -> 28.1 us
    pallas_call x1, Pallas kernels: 23.2 us -> 26.1 us  [body(): pl.pallas_call(functools.partial(exchange_kernel, gx, gy, nx), out_shape=...]
    pallas_call x1, Pallas kernels: 4.06 us -> 1.99 us  [body(): pl.pallas_call(functools.partial(finish_kernel, nx), out_shape=[jax.Shape...]
where the time goes in v3:
time: 29.5 us; the launch traced here: 29.4 us
  Pallas kernels  28.1 us (95%)
  between operations  1.29 us (4%)
    pallas_call x1, Pallas kernels, body(): pl.pallas_call(functools.partial(exchange_kernel, gx, gy, nx), out_shape=...  26.1 us
    pallas_call x1, Pallas kernels, body(): pl.pallas_call(functools.partial(finish_kernel, nx), out_shape=[jax.Shape...  1.99 us

profile of v3, /device:TPU:8, one launch (start us, length us, event | category | flops | bytes accessed | tf_op | source)
XLA Modules:
  0.0 29.4 jit_solution(12218468923395892082)
XLA Ops:
  1.3 26.1 %exchange.1 = (f32[3,17,48,128]{3,2,1,0:T(8,128)S(1)}, f32[3,16,48,128]{3,2,1,0:T(8,128)S(1)}, f32[3,16,48,128]{3,2,1,0:T(8,128)S(1)}, f32[3,16,48,128]{3,2,1,0:...) custom-call(s32[2]{0:T(128)} %pml_in.1, ...), custom_call_target="tpu_custom_call" | custom-call | tf_op jit(solution)/shard_map/exchange/pallas_call | solution.py:384
  27.4 2.0 %finish.1 = (f32[3,16,48,128]{3,2,1,0:T(8,128)}, f32[3,16,48,128]{3,2,1,0:T(8,128)}, f32[3,16,48,128]{3,2,1,0:T(8,128)}, f32[12,16,128]{2,1,0:T(8,128)}) custom-call(f32[3,17,48,128]{3,2,1,0:T(8,128)S(1)} %get-tuple-element.19.e1, f32[3,16,48,128]{3,2,1,0:T(8,128)S(1)} %get-tuple-element.20.h1, f32[3,16,48,128]{3,2,1,0:T(8,128)S(1)} %get-tuple-element.21.j1, ...), custom_call_target="tpu_custom_call" | custom-call | tf_op jit(solution)/shard_map/finish/pallas_call | solution.py:418

commit v4 on v2

--- a/solution.py
+++ b/solution.py
@@ -104,7 +104,7 @@
     return hx, hp[1, x], hz
 
 
-def e_update(x, prev, hp, e, j, mat, col_e, col_h, decay, scale, outs):
+def e_update(x, prev, hp, e, j, mats, col_e, col_h, decay, scale, outs):
     lane = lanes()
     e_out, h_out, j_out = outs
     hy_xp, hz_xp = prev
@@ -115,9 +115,7 @@
     h_out[2, x] = hz
     hx_yp = jnp.where(first, pltpu.roll(col_h, YL - x, 1), pltpu.roll(hx, 1, 1))
     hz_yp = jnp.where(first, pltpu.roll(col_h, YL - GAP - x, 1), pltpu.roll(hz, 1, 1))
-    m = mat[x]
-    metal = m == 2
-    e_scale = scale * jnp.where(m == 1, 0.25, 1.0)
+    e_scale, gain = mats[0, x], mats[1, x]
     backs = (
         hz - hz_yp - (hy - z_prev(hy)),
         hx - z_prev(hx) - (hz - hz_xp),
@@ -125,9 +123,9 @@
     )
     for c, back in enumerate(backs):
         j_now = j[c, x]
-        e_new = decay * e[c, x] + e_scale * (back - jnp.where(metal, j_now, 0.0))
+        e_new = decay * e[c, x] + e_scale * (back - j_now)
         e_out[c, x] = e_new
-        j_out[c, x] = jnp.where(metal, DRUDE_KEEP * j_now + DRUDE_GAIN * e_new, 0.0)
+        j_out[c, x] = DRUDE_KEEP * j_now + gain * e_new
     return hy, hz
 
 
@@ -152,8 +150,8 @@
 def exchange_kernel(
     gx, gy, nx,
     pml_in, tick_in, e_in, h_in, j_in, m_in, f_in,
-    e1, h1, j1, mat, w, grad, coef, rim_x, col_e_out, col_h_out,
-    pml, tick, e0, hp, j0, fwd, pack_e, pack_h, send_h, tile_e, tile_h,
+    e1, h1, j1, mats, w, grad, coef, rim_x, col_e_out, col_h_out,
+    pml, tick, e0, hp, j0, mat, fwd, pack_e, pack_h, send_h, tile_e, tile_h,
     got_e, got_slab, got_h, got_ye, got_yh, got_de, got_dh,
     field_sem, load_sem, send_sem, recv_sem,
 ):
@@ -225,13 +223,15 @@
             copy.start()
         return copies
 
-    def last_plane(level, e, h, h_out):
-        packs = h_partial(nx - 1, e, h, h_out, coef[0], coef[1], (zero, zero))
-        send_h[level, 0] = h_out[1, nx - 1]
-        send_h[level, 1] = h_out[2, nx - 1]
+    def pack(level, packs):
+        pack_e[level] = packs[0]
+        pack_h[level] = packs[1]
+
+    def rim(level, e, h):
+        send_h[level, 0] = h[1, nx - 1]
+        send_h[level, 1] = h[2, nx - 1]
         tile_h[level] = column_to_tile(e[1, 0, :, YL - 1 : YL])
         tile_e[level] = column_to_tile(e[0, nx - 1, :, 0:1])
-        return packs
 
     def receive(level, e, h):
         e[0, nx, pl.ds(W0, WN)] = got_slab[level]
@@ -266,12 +266,8 @@
             functools.partial(plane, e=e0, h=hp, h_out=hp),
             packs,
         )
-    pack_e[0] = packs[0]
-    pack_h[0] = packs[1]
-    send_h[0, 0] = hp[1, nx - 1]
-    send_h[0, 1] = hp[2, nx - 1]
-    tile_h[0] = column_to_tile(e0[1, 0, :, YL - 1 : YL])
-    tile_e[0] = column_to_tile(e0[0, nx - 1, :, 0:1])
+    pack(0, packs)
+    rim(0, e0, hp)
     pl.semaphore_wait(barrier, len(peers))
     copies = send(0, e0, (5, 4, 3, 2, 0, 1, 6))
 
@@ -297,6 +293,17 @@
     lax.fori_loop(0, DZ, weigh, 0)
     late[1].wait()
     late[2].wait()
+
+    def materials(x, carry):
+        m = mat[x]
+        metal = m == 2
+        mats[0, x] = coef[1] * jnp.where(m == 1, 0.25, 1.0)
+        mats[1, x] = jnp.where(metal, DRUDE_GAIN, 0.0)
+        for c in range(3):
+            j0[c, x] = jnp.where(metal, j0[c, x], 0.0)
+        return carry
+
+    lax.fori_loop(0, nx, materials, 0)
     for copy in copies:
         copy.wait()
 
@@ -306,18 +313,18 @@
 
     def advance(x, prev):
         return e_update(
-            x, prev, hp, e0, j0, mat, col_e_out[...], col_h_out[...], coef[0], coef[1], (e1, hp, j1)
+            x, prev, hp, e0, j0, mats, col_e_out[...], col_h_out[...], coef[0], coef[1], (e1, hp, j1)
         )
 
     prev = advance(0, (hy, hz))
     copies = send(1, e1, (0, 1))
     advance(nx - 1, h_full(nx - 2, hp, col_e_out[...], coef[1])[1:])
-    packs = last_plane(1, e1, hp, h1)
+    pack(1, h_partial(nx - 1, e1, hp, h1, coef[0], coef[1], (zero, zero)))
+    rim(1, e1, h1)
     copies += send(1, e1, (2, 5, 6))
     lax.fori_loop(1, nx - 1, advance, prev)
-    packs = lax.fori_loop(0, nx - 1, functools.partial(plane, e=e1, h=hp, h_out=h1), packs)
-    pack_e[1] = packs[0]
-    pack_h[1] = packs[1]
+    packs = (pack_e[1], pack_h[1])
+    pack(1, lax.fori_loop(0, nx - 1, functools.partial(plane, e=e1, h=hp, h_out=h1), packs))
     copies += send(1, e1, (3, 4))
 
     for z in range(DZ):
@@ -333,7 +340,7 @@
 
 def finish_kernel(
     nx,
-    e1, h1, j1, mat, w, grad, coef, rim_x, col_e, col_h,
+    e1, h1, j1, mats, w, grad, coef, rim_x, col_e, col_h,
     e_res, h_res, j_res, g_res,
     e2, h2, j2, g2, sem, g_sem,
 ):
@@ -345,7 +352,7 @@
 
     def advance(x, prev):
         out = e_update(
-            x, prev, h1, e1, j1, mat, col_e[...], col_h[...], coef[0], coef[1], (e2, h2, j2)
+            x, prev, h1, e1, j1, mats, col_e[...], col_h[...], coef[0], coef[1], (e2, h2, j2)
         )
         for copy in copies(x):
             copy.start()
@@ -376,7 +383,7 @@
     hbm = pl.BlockSpec(memory_space=pltpu.HBM)
     vmem = pl.BlockSpec(memory_space=pltpu.VMEM)
     kept = [
-        (padded, F32), (field, F32), (field, F32), ((nx, Z, YL), jnp.int32), ((STEPS, 3, DZ, nx, YL), F32),
+        (padded, F32), (field, F32), (field, F32), ((2, nx, Z, YL), F32), ((STEPS, 3, DZ, nx, YL), F32),
         ((DZ, nx, YL), F32), ((2,) + plane, F32), ((2,) + plane, F32), (plane, F32), (plane, F32),
     ]
     mid = pl.pallas_call(
@@ -390,6 +397,7 @@
             pltpu.VMEM(padded, F32),
             pltpu.VMEM(field, F32),
             pltpu.VMEM(field, F32),
+            pltpu.VMEM((nx, Z, YL), jnp.int32),
             pltpu.VMEM(slab.shape, slab.dtype),
             pltpu.VMEM((STEPS,) + plane, F32),
             pltpu.VMEM((STEPS,) + plane, F32),
@@ -409,7 +417,7 @@
             pltpu.SemaphoreType.DMA((STEPS, 7)),
         ],
         compiler_params=pltpu.CompilerParams(
-            collective_id=0, has_side_effects=True, vmem_limit_bytes=58 << 20
+            collective_id=0, has_side_effects=True, vmem_limit_bytes=57 << 20
         ),
         name="exchange",
     )(pml_cells, time_index, e_field, h_field, current, material, slab)

time: 28.7 us -> 28.7 us (level)
  no operation moved by 1% of the time
where the time goes in v4:
time: 28.7 us; the launch traced here: 28.6 us
  Pallas kernels  27.3 us (95%)
  between operations  1.29 us (4%)
    pallas_call x1, Pallas kernels, body(): pl.pallas_call(functools.partial(exchange_kernel, gx, gy, nx), out_shape=...  23.2 us
    pallas_call x1, Pallas kernels, body(): pl.pallas_call(functools.partial(finish_kernel, nx), out_shape=[jax.Shape...  4.05 us

profile of v4, /device:TPU:8, one launch (start us, length us, event | category | flops | bytes accessed | tf_op | source)
XLA Modules:
  0.0 28.6 jit_solution(7727868504503156615)
XLA Ops:
  1.3 23.2 %exchange.1 = (f32[3,17,48,128]{3,2,1,0:T(8,128)S(1)}, f32[3,16,48,128]{3,2,1,0:T(8,128)S(1)}, f32[3,16,48,128]{3,2,1,0:T(8,128)S(1)}, f32[2,16,48,128]{3,2,1,0:...) custom-call(s32[2]{0:T(128)} %pml_in.1, ...), custom_call_target="tpu_custom_call" | custom-call | tf_op jit(solution)/shard_map/exchange/pallas_call | solution.py:389
  24.5 4.1 %finish.1 = (f32[3,16,48,128]{3,2,1,0:T(8,128)}, f32[3,16,48,128]{3,2,1,0:T(8,128)}, f32[3,16,48,128]{3,2,1,0:T(8,128)}, f32[12,16,128]{2,1,0:T(8,128)}) custom-call(f32[3,17,48,128]{3,2,1,0:T(8,128)S(1)} %get-tuple-element.18.e1, f32[3,16,48,128]{3,2,1,0:T(8,128)S(1)} %get-tuple-element.19.h1, f32[3,16,48,128]{3,2,1,0:T(8,128)S(1)} %get-tuple-element.20.j1, ...), custom_call_target="tpu_custom_call" | custom-call | tf_op jit(solution)/shard_map/finish/pallas_call | solution.py:424

commit v5 on v4

--- a/solution.py
+++ b/solution.py
@@ -344,33 +344,27 @@
     e_res, h_res, j_res, g_res,
     e2, h2, j2, g2, sem, g_sem,
 ):
-    def copies(x):
-        return [
-            pltpu.make_async_copy(src.at[:, x], dst.at[:, x], sem.at[i, x])
-            for i, (src, dst) in enumerate(((e2, e_res), (h2, h_res), (j2, j_res)))
-        ]
+    size = nx // CHUNKS
+    copies = []
 
     def advance(x, prev):
-        out = e_update(
+        return e_update(
             x, prev, h1, e1, j1, mats, col_e[...], col_h[...], coef[0], coef[1], (e2, h2, j2)
         )
-        for copy in copies(x):
-            copy.start()
-        return out
-
-    lax.fori_loop(0, nx, advance, (rim_x[0], rim_x[1]))
+
+    prev = (rim_x[0], rim_x[1])
+    for n in range(CHUNKS):
+        prev = lax.fori_loop(n * size, (n + 1) * size, advance, prev)
+        span = pl.ds(n * size, size)
+        for i, (src, dst) in enumerate(((e2, e_res), (h2, h_res), (j2, j_res))):
+            copies.append(pltpu.make_async_copy(src.at[:, span], dst.at[:, span], sem.at[i, n]))
+            copies[-1].start()
     for z in range(DZ):
         g2[z] = grad[z] + slab_grad(z, e1, col_e, w, 1)
-    g_copy = pltpu.make_async_copy(g2, g_res, g_sem)
-    g_copy.start()
-
-    def drain(x, carry):
-        for copy in copies(x):
-            copy.wait()
-        return carry
-
-    lax.fori_loop(0, nx, drain, 0)
-    g_copy.wait()
+    copies.append(pltpu.make_async_copy(g2, g_res, g_sem))
+    copies[-1].start()
+    for copy in copies:
+        copy.wait()
 
 
 def body(gx, gy, e_field, h_field, current, material, pml_cells, forward_field, time_index):
@@ -436,7 +430,7 @@
             pltpu.VMEM(field, F32),
             pltpu.VMEM(field, F32),
             pltpu.VMEM((DZ, nx, YL), F32),
-            pltpu.SemaphoreType.DMA((3, nx)),
+            pltpu.SemaphoreType.DMA((3, CHUNKS)),
             pltpu.SemaphoreType.DMA(()),
         ],
         compiler_params=pltpu.CompilerParams(vmem_limit_bytes=24 << 20),

time: 28.7 us -> 28.5 us (level)
  no operation moved by 1% of the time
where the time goes in v5:
time: 28.5 us; the launch traced here: 28.4 us
  Pallas kernels  27.1 us (95%)
  between operations  1.29 us (5%)
    pallas_call x1, Pallas kernels, body(): pl.pallas_call(functools.partial(exchange_kernel, gx, gy, nx), out_shape=...  23.2 us
    pallas_call x1, Pallas kernels, body(): pl.pallas_call(functools.partial(finish_kernel, nx), out_shape=[jax.Shape...  3.91 us

profile of v5, /device:TPU:8, one launch (start us, length us, event | category | flops | bytes accessed | tf_op | source)
XLA Modules:
  0.0 28.4 jit_solution(15181690427324381731)
XLA Ops:
  1.3 23.2 %exchange.1 = (f32[3,17,48,128]{3,2,1,0:T(8,128)S(1)}, f32[3,16,48,128]{3,2,1,0:T(8,128)S(1)}, f32[3,16,48,128]{3,2,1,0:T(8,128)S(1)}, f32[2,16,48,128]{3,2,1,0:...) custom-call(s32[2]{0:T(128)} %pml_in.1, ...), custom_call_target="tpu_custom_call" | custom-call | tf_op jit(solution)/shard_map/exchange/pallas_call | solution.py:383
  24.5 3.9 %finish.1 = (f32[3,16,48,128]{3,2,1,0:T(8,128)}, f32[3,16,48,128]{3,2,1,0:T(8,128)}, f32[3,16,48,128]{3,2,1,0:T(8,128)}, f32[12,16,128]{2,1,0:T(8,128)}) custom-call(f32[3,17,48,128]{3,2,1,0:T(8,128)S(1)} %get-tuple-element.18.e1, f32[3,16,48,128]{3,2,1,0:T(8,128)S(1)} %get-tuple-element.19.h1, f32[3,16,48,128]{3,2,1,0:T(8,128)S(1)} %get-tuple-element.20.j1, ...), custom_call_target="tpu_custom_call" | custom-call | tf_op jit(solution)/shard_map/finish/pallas_call | solution.py:418
